TPU v7x, 128 devices: a whole 4x4x4 slice. The times are simulated.
128 devices in a mesh: group: 4 (over x), chan: 32 (over y, z, core).
Axes of the slice: x: 4, y: 4, z: 4, core: 2. Of those that a mesh axis runs over, the one named last changes fastest.
Arguments:
- generator: bfloat16 [256, 768, 768], P(('group', 'chan')), may hold values from -0.21875 to 0.21875
- hamiltonian: bfloat16 [256, 768, 768], P(('group', 'chan')), may hold values from -6 to 6
- pair_weight: float32 [256, 768], P(('group', 'chan')), may hold values from -1 to 1
- cross_weight: float32 [256, 768], P(('group', 'chan')), may hold values from -1 to 1
- channel_size: int32 [256], P(('group', 'chan')), may hold values from 1 to 768, as said below
- send_table: int32 [128, 1664], P(('group', 'chan')), may hold values from 0 to 1152, as said below
- receive_table: int32 [128, 1664], P(('group', 'chan')), may hold values from 0 to 1152, as said below
Outputs:
- new_hamiltonian: float32 [256, 768, 768], P(('group', 'chan'))
Inputs may be any that keep to these rules, and one draw needn't show every extreme that they name: `channel_size`: at least one channel has exactly 768. `send_table`: value 1152 marks an empty slot; in each device's row the filled slots toward one destination come first and name every local tile exactly once; some pair of devices uses all 13 slots. `receive_table`: value 1152 marks an empty slot; slot (s, k) of device r is filled exactly when slot (r, k) of device s in send_table is; the filled slots name every local particle-hole tile exactly once.
All inputs are finite; a program needn't handle non-finite values.
Results may differ from a plain program's by a relative error of at most 0.0011.
Values may be sent and summed in bfloat16 or wider, within the bound.
No kernel may reach another device: no remote copies, remote signals or barrier semaphores. Data moves between devices by JAX's collectives and lax.ppermute only.
A program may use at most 128 MiB of HBM per device.

v0:
```python
import jax
import jax.numpy as jnp
from jax import lax
from jax.sharding import PartitionSpec as P

TILE = 32


flow_step = 0.5


def commutator(former, latter, weight):
    latter_weighted = (weight[:, :, None] * latter.astype(jnp.float32)).astype(jnp.bfloat16)
    former_weighted = (weight[:, :, None] * former.astype(jnp.float32)).astype(jnp.bfloat16)
    first = jnp.einsum("cij,cjk->cik", former, latter_weighted, preferred_element_type=jnp.float32)
    second = jnp.einsum("cij,cjk->cik", latter, former_weighted, preferred_element_type=jnp.float32)
    return first - second


def inverse_of(table_row, tile_count):
    slots = jnp.arange(table_row.shape[0], dtype=jnp.int32)
    return jnp.zeros((tile_count + 1,), jnp.int32).at[table_row].set(slots)[:tile_count]


def per_device(
    generator, hamiltonian, pair_weight, cross_weight, channel_size, send_table, receive_table
):
    channels, extent, _ = generator.shape
    tile_count = channels * (extent // TILE) ** 2
    columns = lax.broadcasted_iota(jnp.int32, (channels, extent), 1)
    inside = columns < channel_size[:, None]
    window = inside[:, :, None] & inside[:, None, :]
    blank = jnp.zeros((), jnp.bfloat16)
    masked_generator = jnp.where(window, generator, blank)
    masked_hamiltonian = jnp.where(window, hamiltonian, blank)
    send_row = send_table[0]
    receive_row = receive_table[0]
    send_pick = jnp.minimum(send_row, tile_count - 1)
    outgoing_generator = masked_generator.reshape(tile_count, TILE * TILE)[send_pick]
    outgoing_hamiltonian = masked_hamiltonian.reshape(tile_count, TILE * TILE)[send_pick]
    arrived_generator, arrived_hamiltonian = (
        lax.all_to_all(
            outgoing_generator, ("group", "chan"), split_axis=0, concat_axis=0, tiled=True
        ),
        lax.all_to_all(
            outgoing_hamiltonian, ("group", "chan"), split_axis=0, concat_axis=0, tiled=True
        ),
    )
    ladder = commutator(masked_generator, masked_hamiltonian, pair_weight)
    arrival_slot = inverse_of(receive_row, tile_count)
    cross_generator = arrived_generator[arrival_slot].reshape(channels, extent, extent)
    cross_hamiltonian = arrived_hamiltonian[arrival_slot].reshape(channels, extent, extent)
    crossed = commutator(cross_generator, cross_hamiltonian, cross_weight).astype(jnp.bfloat16)
    going_back = crossed.reshape(tile_count, TILE * TILE)[jnp.minimum(receive_row, tile_count - 1)]
    came_back = lax.all_to_all(
        going_back, ("group", "chan"), split_axis=0, concat_axis=0, tiled=True
    )
    returned = came_back[inverse_of(send_row, tile_count)].reshape(channels, extent, extent)
    summed = masked_hamiltonian.astype(jnp.float32) + flow_step * (
        ladder + returned.astype(jnp.float32)
    )
    return jnp.where(window, summed, jnp.zeros((), jnp.float32))


def solution(mesh):
    in_specs = (
        P(("group", "chan"), None, None),
        P(("group", "chan"), None, None),
        P(("group", "chan"), None),
        P(("group", "chan"), None),
        P(("group", "chan")),
        P(("group", "chan"), None),
        P(("group", "chan"), None),
    )
    out_specs = P(("group", "chan"), None, None)
    return jax.shard_map(
        per_device, mesh=mesh, in_specs=in_specs, out_specs=out_specs, check_vma=False
    )
```

profile of v0, /device:TPU:1, one launch (start us, length us, event | category | flops | bytes accessed | tf_op | source)
XLA Modules:
  0.0 265.3 jit_solution(14963033412192818867)
XLA Ops:
  0.0 0.7 iota_compare_fusion
  0.7 0.7 fusion.15
  1.5 4.4 %and_select_fusion.1 = (bf16[2,768,768]{2,1,0:T(8,128)(2,1)}, bf16[2,768,768]{2,1,0:T(8,128)(2,1)}) fusion(bf16[2,768,768]{2,1,0:T(8,128)(2,1)} %param.7, pred[2,768]{1,0:T(4,128)(4,1)S(1)} %iota_compare_fusion, bf16[2,768,768]{2,1,0:T(8,128)(2,1)} %param.8), kind=kLoop, calls=%fused_computation.9 | loop fusion | flops 3538944 | bytes 9438720 | tf_op jit(solution)/shard_map/jit(_where)/select_n | solution.py:34
  5.9 4.1 %reshape.152 = bf16[1152,1024]{1,0:T(8,128)(2,1)S(1)} reshape(bf16[2,768,768]{2,1,0:T(8,128)(2,1)} %get-tuple-element.9) | data formatting | bytes 4718592 | tf_op jit(solution)/shard_map/reshape | solution.py:39
  10.0 6.5 %gather_fusion = bf16[1664,1024]{1,0:T(8,128)(2,1)} fusion(bf16[1152,1024]{1,0:T(8,128)(2,1)S(1)} %reshape.152, s32[2048]{0:T(1024)S(1)} %pad_clamp_fusion.3), kind=kCustom, calls=%fused_computation | custom fusion | bytes 6822400 | tf_op jit(solution)/shard_map/gather | solution.py:39
  16.5 5.8 %all_to_all.24 = bf16[128,13,1024]{2,1,0:T(8,128)(2,1)} reshape(bf16[1664,1024]{1,0:T(8,128)(2,1)} %gather_fusion) | data formatting | bytes 6815744 | tf_op jit(solution)/shard_map/all_to_all | solution.py:42
  22.3 11.9 %all-to-all-start = ((bf16[128,13,1024]{2,1,0:T(8,128)(2,1)}), bf16[128,13,1024]{2,1,0:T(8,128)(2,1)}, u32[]{:S(2)}, u32[]{:S(2)}) async-start(bf16[128,13,1024]{2,1,0:T(8,128)(2,1)} %all_to_all.24), calls=%async_computation | async-start | bytes 8388608 | tf_op jit(solution)/shard_map/all_to_all | solution.py:42
  34.2 4.1 %reshape.154 = bf16[1152,1024]{1,0:T(8,128)(2,1)S(1)} reshape(bf16[2,768,768]{2,1,0:T(8,128)(2,1)} %get-tuple-element.10) | data formatting | bytes 4718592 | tf_op jit(solution)/shard_map/reshape | solution.py:40
  38.3 6.6 %gather_fusion.2 = bf16[1664,1024]{1,0:T(8,128)(2,1)} fusion(bf16[1152,1024]{1,0:T(8,128)(2,1)S(1)} %reshape.154, s32[2048]{0:T(1024)S(1)} %pad_clamp_fusion.3), kind=kCustom, calls=%fused_computation.2 | custom fusion | bytes 6822400 | tf_op jit(solution)/shard_map/gather | solution.py:40
  44.9 5.8 %all_to_all.27 = bf16[128,13,1024]{2,1,0:T(8,128)(2,1)} reshape(bf16[1664,1024]{1,0:T(8,128)(2,1)} %gather_fusion.2) | data formatting | bytes 6815744 | tf_op jit(solution)/shard_map/all_to_all | solution.py:45
  50.7 0.0 copy-start.5
  50.7 36.2 %all-to-all-done = bf16[128,13,1024]{2,1,0:T(8,128)(2,1)} async-done(((bf16[128,13,1024]{2,1,0:T(8,128)(2,1)}), bf16[128,13,1024]{2,1,0:T(8,128)(2,1)}, u32[]{:S(2)}, u32[]{:S(2)}) %all-to-all-start) | async-done | bytes 3407904 | tf_op jit(solution)/shard_map/all_to_all | solution.py:42
  86.9 5.7 %all-to-all-start.1 = ((bf16[128,13,1024]{2,1,0:T(8,128)(2,1)}), bf16[128,13,1024]{2,1,0:T(8,128)(2,1)}, u32[]{:S(2)}, u32[]{:S(2)}) async-start(bf16[128,13,1024]{2,1,0:T(8,128)(2,1)} %all_to_all.27), calls=%async_computation.1 | async-start | bytes 8388608 | tf_op jit(solution)/shard_map/all_to_all | solution.py:45
  92.6 0.0 copy-done.5
  92.7 9.0 %scatter_custom_fusion = s32[1153]{0:T(1024)S(1)} fusion(s32[1664]{0:T(1024)S(1)} %get-tuple-element.8, s32[1664]{0:T(1024)S(1)} %iota.16, s32[]{:T(128)} %constant.0.clone.1), kind=kCustom, calls=%fused_computation.45 | custom fusion | bytes 4616 | tf_op jit(solution)/shard_map/scatter | solution.py:22
  101.7 4.2 %all_to_all.26 = bf16[1664,1024]{1,0:T(8,128)(2,1)S(1)} reshape(bf16[128,13,1024]{2,1,0:T(8,128)(2,1)} %all-to-all-done) | data formatting | bytes 6815744 | tf_op jit(solution)/shard_map/all_to_all | solution.py:42
  106.0 5.0 %gather_fusion.1 = bf16[1152,1024]{1,0:T(8,128)(2,1)} fusion(bf16[1664,1024]{1,0:T(8,128)(2,1)S(1)} %all_to_all.26, s32[2048]{0:T(1024)S(1)} %pad_clamp_fusion.2), kind=kCustom, calls=%fused_computation.1 | custom fusion | bytes 4723200 | tf_op jit(solution)/shard_map/gather | solution.py:51
  111.0 5.2 %reshape.153 = bf16[2,768,768]{2,1,0:T(8,128)(2,1)} reshape(bf16[1152,1024]{1,0:T(8,128)(2,1)} %gather_fusion.1) | data formatting | bytes 4718592 | tf_op jit(solution)/shard_map/reshape | solution.py:51
  116.1 29.4 %all-to-all-done.1 = bf16[128,13,1024]{2,1,0:T(8,128)(2,1)} async-done(((bf16[128,13,1024]{2,1,0:T(8,128)(2,1)}), bf16[128,13,1024]{2,1,0:T(8,128)(2,1)}, u32[]{:S(2)}, u32[]{:S(2)}) %all-to-all-start.1) | async-done | bytes 3407904 | tf_op jit(solution)/shard_map/all_to_all | solution.py:45
  145.5 4.2 %all_to_all.29 = bf16[1664,1024]{1,0:T(8,128)(2,1)S(1)} reshape(bf16[128,13,1024]{2,1,0:T(8,128)(2,1)} %all-to-all-done.1) | data formatting | bytes 6815744 | tf_op jit(solution)/shard_map/all_to_all | solution.py:45
  149.7 5.0 %gather_fusion.3 = bf16[1152,1024]{1,0:T(8,128)(2,1)} fusion(bf16[1664,1024]{1,0:T(8,128)(2,1)S(1)} %all_to_all.29, s32[2048]{0:T(1024)S(1)} %pad_clamp_fusion.2), kind=kCustom, calls=%fused_computation.3 | custom fusion | bytes 4723200 | tf_op jit(solution)/shard_map/gather | solution.py:52
  154.7 0.0 copy-start.2
  154.7 0.0 copy-start.6
  154.7 5.3 %reshape.155 = bf16[2,768,768]{2,1,0:T(8,128)(2,1)} reshape(bf16[1152,1024]{1,0:T(8,128)(2,1)} %gather_fusion.3) | data formatting | bytes 4718592 | tf_op jit(solution)/shard_map/reshape | solution.py:52
  160.0 0.0 copy-done.2
  160.0 0.0 copy-done.6
  160.0 0.0 copy-start.3
  160.0 3.9 %fusion.2 = f32[2,768,768]{2,1,0:T(8,128)S(1)} fusion(bf16[2,768,768]{2,1,0:T(8,128)(2,1)S(1)} %copy-done.2, bf16[2,768,768]{2,1,0:T(8,128)(2,1)} %reshape.155, f32[2,768]{1,0:T(2,128)S(1)} %copy-done.6), kind=kOutput, calls=%fused_computation.19 | convolution fusion | flops 1815478272 | bytes 9443328 | tf_op jit(solution)/shard_map/cij,cjk->cik/dot_general | solution.py:15
  163.9 0.0 copy-done.3
  163.9 3.6 %subtract_convert_fusion = bf16[2,768,768]{2,1,0:T(8,128)(2,1)} fusion(f32[2,768,768]{2,1,0:T(8,128)S(1)} %fusion.2, bf16[2,768,768]{2,1,0:T(8,128)(2,1)S(1)} %copy-done.3, bf16[2,768,768]{2,1,0:T(8,128)(2,1)S(1)} %copy-done.2, f32[2,768]{1,0:T(2,128)S(1)} %copy-done.6), kind=kOutput, calls=%fused_computation.14 | convolution fusion | flops 1817837568 | bytes 11802624 | tf_op jit(solution)/shard_map/cij,cjk->cik/dot_general | solution.py:16
  167.5 4.1 %reshape.156 = bf16[1152,1024]{1,0:T(8,128)(2,1)S(1)} reshape(bf16[2,768,768]{2,1,0:T(8,128)(2,1)} %subtract_convert_fusion) | data formatting | bytes 4718592 | tf_op jit(solution)/shard_map/reshape | solution.py:54
  171.6 6.5 %gather_fusion.4 = bf16[1664,1024]{1,0:T(8,128)(2,1)} fusion(bf16[1152,1024]{1,0:T(8,128)(2,1)S(1)} %reshape.156, s32[2048]{0:T(1024)S(1)} %pad_clamp_fusion.1), kind=kCustom, calls=%fused_computation.4 | custom fusion | bytes 6822400 | tf_op jit(solution)/shard_map/gather | solution.py:54
  178.1 5.8 %all_to_all.30 = bf16[128,13,1024]{2,1,0:T(8,128)(2,1)} reshape(bf16[1664,1024]{1,0:T(8,128)(2,1)} %gather_fusion.4) | data formatting | bytes 6815744 | tf_op jit(solution)/shard_map/all_to_all | solution.py:55
  183.9 0.0 copy-start
  183.9 0.0 copy-start.4
  183.9 5.9 %all-to-all-start.2 = ((bf16[128,13,1024]{2,1,0:T(8,128)(2,1)}), bf16[128,13,1024]{2,1,0:T(8,128)(2,1)}, u32[]{:S(2)}, u32[]{:S(2)}) async-start(bf16[128,13,1024]{2,1,0:T(8,128)(2,1)} %all_to_all.30), calls=%async_computation.2 | async-start | bytes 8388608 | tf_op jit(solution)/shard_map/all_to_all | solution.py:55
  189.8 9.0 %scatter_custom_fusion.1 = s32[1153]{0:T(1024)S(1)} fusion(s32[1664]{0:T(1024)S(1)} %get-tuple-element.5, s32[1664]{0:T(1024)S(1)} %iota.17, s32[]{:T(128)} %constant.0.clone.1), kind=kCustom, calls=%fused_computation.43 | custom fusion | bytes 4616 | tf_op jit(solution)/shard_map/scatter | solution.py:22
  198.8 0.0 copy-done
  198.8 0.0 copy-done.4
  198.8 5.9 %fusion.1 = f32[2,768,768]{2,1,0:T(8,128)} fusion(bf16[2,768,768]{2,1,0:T(8,128)(2,1)} %get-tuple-element.10, bf16[2,768,768]{2,1,0:T(8,128)(2,1)S(1)} %copy-done, f32[2,768]{1,0:T(2,128)S(1)} %copy-done.4), kind=kOutput, calls=%fused_computation.18 | convolution fusion | flops 1815478272 | bytes 9443328 | tf_op jit(solution)/shard_map/cij,cjk->cik/dot_general | solution.py:16
  204.7 37.9 %all-to-all-done.2 = bf16[128,13,1024]{2,1,0:T(8,128)(2,1)} async-done(((bf16[128,13,1024]{2,1,0:T(8,128)(2,1)}), bf16[128,13,1024]{2,1,0:T(8,128)(2,1)}, u32[]{:S(2)}, u32[]{:S(2)}) %all-to-all-start.2) | async-done | bytes 3407904 | tf_op jit(solution)/shard_map/all_to_all | solution.py:55
  242.6 4.2 %all_to_all.32 = bf16[1664,1024]{1,0:T(8,128)(2,1)S(1)} reshape(bf16[128,13,1024]{2,1,0:T(8,128)(2,1)} %all-to-all-done.2) | data formatting | bytes 6815744 | tf_op jit(solution)/shard_map/all_to_all | solution.py:55
  246.8 5.0 %gather_fusion.5 = bf16[1152,1024]{1,0:T(8,128)(2,1)} fusion(bf16[1664,1024]{1,0:T(8,128)(2,1)S(1)} %all_to_all.32, s32[2048]{0:T(1024)S(1)} %pad_clamp_fusion), kind=kCustom, calls=%fused_computation.5 | custom fusion | bytes 4723200 | tf_op jit(solution)/shard_map/gather | solution.py:58
  251.9 0.0 copy-start.1
  251.9 5.5 %reshape.157 = f32[2,768,768]{2,1,0:T(8,128)} reshape(bf16[1152,1024]{1,0:T(8,128)(2,1)} %gather_fusion.5) | data formatting | bytes 7077888 | tf_op jit(solution)/shard_map/convert_element_type | solution.py:60
  257.3 0.0 copy-done.1
  257.4 7.9 %and_select_fusion = f32[2,768,768]{2,1,0:T(8,128)} fusion(bf16[2,768,768]{2,1,0:T(8,128)(2,1)} %get-tuple-element.10, f32[2,768,768]{2,1,0:T(8,128)} %reshape.157, f32[2,768,768]{2,1,0:T(8,128)} %fusion.1, pred[2,768]{1,0:T(4,128)(4,1)S(1)} %iota_compare_fusion, bf16[2,768,768]{2,1,0:T(8,128)(2,1)S(1)} %copy-done.1, f32[2,768]{1,0:T(2,128)S(1)} %copy-done.4), kind=kOutput, calls=%fused_computation.8 | convolution fusion | flops 1823735808 | bytes 18882048 | tf_op jit(solution)/shard_map/cij,cjk->cik/dot_general | solution.py:15
  (9 shorter events, 0.1 us)
Async XLA Ops:
  22.3 64.7 %all-to-all-start = ((bf16[128,13,1024]{2,1,0:T(8,128)(2,1)}), bf16[128,13,1024]{2,1,0:T(8,128)(2,1)}, u32[]{:S(2)}, u32[]{:S(2)}) async-start(bf16[128,13,1024]{2,1,0:T(8,128)(2,1)} %all_to_all.24), calls=%async_computation | async-start | bytes 8388608 | tf_op jit(solution)/shard_map/all_to_all | solution.py:42
  50.7 41.9 %copy-start.5 = (s32[1,1664]{1,0:T(1,128)S(1)}, s32[1,1664]{1,0:T(1,128)}, u32[]{:S(2)}) copy-start(s32[1,1664]{1,0:T(1,128)} %param.13) | copy-start | bytes 19972
  86.9 58.5 %all-to-all-start.1 = ((bf16[128,13,1024]{2,1,0:T(8,128)(2,1)}), bf16[128,13,1024]{2,1,0:T(8,128)(2,1)}, u32[]{:S(2)}, u32[]{:S(2)}) async-start(bf16[128,13,1024]{2,1,0:T(8,128)(2,1)} %all_to_all.27), calls=%async_computation.1 | async-start | bytes 8388608 | tf_op jit(solution)/shard_map/all_to_all | solution.py:45
  154.7 5.3 %copy-start.2 = (bf16[2,768,768]{2,1,0:T(8,128)(2,1)S(1)}, bf16[2,768,768]{2,1,0:T(8,128)(2,1)}, u32[]{:S(2)}) copy-start(bf16[2,768,768]{2,1,0:T(8,128)(2,1)} %reshape.153) | copy-start | bytes 7077892
  154.7 5.3 %copy-start.6 = (f32[2,768]{1,0:T(2,128)S(1)}, f32[2,768]{1,0:T(2,128)}, u32[]{:S(2)}) copy-start(f32[2,768]{1,0:T(2,128)} %param.10) | copy-start | bytes 18436
  160.0 3.9 %copy-start.3 = (bf16[2,768,768]{2,1,0:T(8,128)(2,1)S(1)}, bf16[2,768,768]{2,1,0:T(8,128)(2,1)}, u32[]{:S(2)}) copy-start(bf16[2,768,768]{2,1,0:T(8,128)(2,1)} %reshape.155) | copy-start | bytes 7077892
  183.9 14.9 %copy-start = (bf16[2,768,768]{2,1,0:T(8,128)(2,1)S(1)}, bf16[2,768,768]{2,1,0:T(8,128)(2,1)}, u32[]{:S(2)}) copy-start(bf16[2,768,768]{2,1,0:T(8,128)(2,1)} %get-tuple-element.9) | copy-start | bytes 7077892
  183.9 14.9 %copy-start.4 = (f32[2,768]{1,0:T(2,128)S(1)}, f32[2,768]{1,0:T(2,128)}, u32[]{:S(2)}) copy-start(f32[2,768]{1,0:T(2,128)} %param.9) | copy-start | bytes 18436
  183.9 58.7 %all-to-all-start.2 = ((bf16[128,13,1024]{2,1,0:T(8,128)(2,1)}), bf16[128,13,1024]{2,1,0:T(8,128)(2,1)}, u32[]{:S(2)}, u32[]{:S(2)}) async-start(bf16[128,13,1024]{2,1,0:T(8,128)(2,1)} %all_to_all.30), calls=%async_computation.2 | async-start | bytes 8388608 | tf_op jit(solution)/shard_map/all_to_all | solution.py:55
  251.9 5.5 %copy-start.1 = (bf16[2,768,768]{2,1,0:T(8,128)(2,1)S(1)}, bf16[2,768,768]{2,1,0:T(8,128)(2,1)}, u32[]{:S(2)}) copy-start(bf16[2,768,768]{2,1,0:T(8,128)(2,1)} %get-tuple-element.9) | copy-start | bytes 7077892
where the time goes:
time: 267 us; the launch traced here: 265 us
  local copies, waits for them, and re-layouts  111 us (42%)
  waiting for transfers between devices  103 us (39%)
  starting transfers between devices  23.5 us (9%)
  matrix products  21.3 us (8%)
  other arithmetic  5.93 us (2%)
    all_to_all x1, waiting for transfers between devices, per_device(): lax.all_to_all(going_back, ('group', 'chan'), split_axis=0, concat_axis=0...  37.9 us
    all_to_all x1, waiting for transfers between devices, per_device(): lax.all_to_all(outgoing_generator, ('group', 'chan'), split_axis=0, conca...  36.2 us
    all_to_all x1, waiting for transfers between devices, per_device(): lax.all_to_all(outgoing_hamiltonian, ('group', 'chan'), split_axis=0, con...  29.4 us
    scatter x2, local copies, waits for them, and re-layouts, inverse_of(): jnp.zeros((tile_count + 1,), jnp.int32).at[table_row].set(slots)  18 us
    all_to_all x1, starting transfers between devices, per_device(): lax.all_to_all(outgoing_generator, ('group', 'chan'), split_axis=0, conca...  11.9 us
    dot_general x2, matrix products, commutator(): jnp.einsum('cij,cjk->cik', former, latter_weighted, preferred_element_typ...  11.8 us
    all_to_all x2, local copies, waits for them, and re-layouts, per_device(): lax.all_to_all(outgoing_generator, ('group', 'chan'), split_axis=0, conca...  10.1 us
    all_to_all x2, local copies, waits for them, and re-layouts, per_device(): lax.all_to_all(outgoing_hamiltonian, ('group', 'chan'), split_axis=0, con...  10 us
  transfers between devices with their start and end apart: 3, of which 3 were waited for; matrix products, arithmetic and copies ran while one was open for 17% of the time, Pallas kernels for 0%

commit v1 on v0

v1 whole, which is shorter than its diff:
```python
import functools

import jax
import jax.numpy as jnp
from jax import lax
from jax.experimental import pallas as pl
from jax.experimental.pallas import tpu as pltpu
from jax.sharding import PartitionSpec as P

TILE = 32
LANES = 128
TROWS = TILE * TILE // LANES
ROWS = 16

flow_step = 0.5

VMEM_LIMIT = 60 * 1024 * 1024
AXES = ("group", "chan")


def params():
    return pltpu.CompilerParams(vmem_limit_bytes=VMEM_LIMIT)


def chunks_of(total, count):
    while total % count:
        count -= 1
    return count, total // count


def loop(count, body, unroll=1):
    lax.fori_loop(0, count, lambda i, _: (body(i), 0)[1], 0, unroll=unroll)


def inside_of(first_row, rows, columns, size):
    row = lax.broadcasted_iota(jnp.int32, (rows, columns), 0) + first_row
    column = lax.broadcasted_iota(jnp.int32, (rows, columns), 1)
    return (row < size) & (column < size)


def spread(weight_row, out_ref):
    extent = weight_row.shape[1]
    for k in range(extent // LANES):
        piece = weight_row[:, k * LANES : (k + 1) * LANES]
        out_ref[k * LANES : (k + 1) * LANES, :] = jnp.transpose(
            jnp.broadcast_to(piece, (LANES, LANES))
        )


def pack_kernel(size_ref, table_ref, gen_hbm, ham_hbm, out_hbm, gen, ham, gen_rows, ham_rows, out, in_sem, out_sem):
    channels, extent, _ = gen.shape
    slots = out.shape[0]
    panels = extent // LANES
    parts, part_rows = chunks_of(extent, 2)
    out_parts, out_slots = chunks_of(slots, out_sem.shape[0])

    def loads(c, h):
        at = pl.ds(h * part_rows, part_rows)
        k = c * parts + h
        return (
            pltpu.make_async_copy(gen_hbm.at[c, at], gen.at[c, at], in_sem.at[0, k]),
            pltpu.make_async_copy(ham_hbm.at[c, at], ham.at[c, at], in_sem.at[1, k]),
        )

    for c in range(channels):
        for h in range(parts):
            for copy in loads(c, h):
                copy.start()
    for c in range(channels):
        size = size_ref[c]
        for h in range(parts):
            for copy in loads(c, h):
                copy.wait()

            def block(b, c=c, h=h, size=size):
                first = pl.multiple_of(h * part_rows + b * ROWS, ROWS)
                inside = inside_of(first, ROWS, extent, size)
                base = (c * extent + first) * panels
                for source, target in ((gen, gen_rows), (ham, ham_rows)):
                    values = source[c, pl.ds(first, ROWS), :].astype(jnp.float32)
                    values = jnp.where(inside, values, 0.0)
                    for p in range(panels):
                        target[pl.ds(base + p, ROWS, stride=panels), :] = values[
                            :, p * LANES : (p + 1) * LANES
                        ]

            loop(part_rows // ROWS, block, unroll=2)

    def store(q):
        at = pl.ds(q * out_slots, out_slots)
        return pltpu.make_async_copy(out.at[at], out_hbm.at[at], out_sem.at[q])

    for q in range(out_parts):

        def pick(j, q=q):
            slot = q * out_slots + j
            at = pl.ds(pl.multiple_of(table_ref[0, slot] * TROWS, TROWS), TROWS)
            out[slot] = jnp.concatenate([gen_rows[at, :], ham_rows[at, :]], axis=0).astype(
                jnp.bfloat16
            )

        loop(out_slots, pick, unroll=16)
        store(q).start()
    for q in range(out_parts):
        store(q).wait()


def cross_kernel(table_ref, weight_ref, in_hbm, out_hbm, arrived, gen_rows, ham_rows, gen, ham, wgen, wham, spread_weight, crossed_rows, out, in_sem, out_sem):
    channels, extent = weight_ref.shape
    slots = out.shape[0]
    panels = extent // LANES
    parts, part_slots = chunks_of(slots, in_sem.shape[0])

    def load(q):
        at = pl.ds(q * part_slots, part_slots)
        return pltpu.make_async_copy(in_hbm.at[at], arrived.at[at], in_sem.at[q])

    for q in range(parts):
        load(q).start()
    for c in range(channels):
        spread(weight_ref[c : c + 1, :], spread_weight.at[c])
    for q in range(parts):
        load(q).wait()

        def place(j, q=q):
            slot = q * part_slots + j
            at = pl.ds(pl.multiple_of(table_ref[0, slot] * TROWS, TROWS), TROWS)
            both = arrived[slot].astype(jnp.float32)
            gen_rows[at, :] = both[:TROWS]
            ham_rows[at, :] = both[TROWS:]

        loop(part_slots, place, unroll=16)
    for c in range(channels):

        def block(b, c=c):
            first = pl.multiple_of(b * ROWS, ROWS)
            rows = pl.ds(first, ROWS)
            base = (c * extent + first) * panels
            weight = spread_weight[c, rows, :]
            for p in range(panels):
                lanes = slice(p * LANES, (p + 1) * LANES)
                g = gen_rows[pl.ds(base + p, ROWS, stride=panels), :]
                h = ham_rows[pl.ds(base + p, ROWS, stride=panels), :]
                gen[rows, lanes] = g.astype(jnp.bfloat16)
                ham[rows, lanes] = h.astype(jnp.bfloat16)
                wgen[rows, lanes] = (weight * g).astype(jnp.bfloat16)
                wham[rows, lanes] = (weight * h).astype(jnp.bfloat16)

        loop(extent // ROWS, block, unroll=2)
        wide = 2 * LANES
        for n in range(extent // wide):
            columns = slice(n * wide, (n + 1) * wide)
            first = jnp.dot(gen[...], wham[:, columns], preferred_element_type=jnp.float32)
            second = jnp.dot(ham[...], wgen[:, columns], preferred_element_type=jnp.float32)
            product = first - second
            for i in range(wide // LANES):
                p = n * (wide // LANES) + i
                crossed_rows[
                    pl.ds(c * extent * panels + p, extent, stride=panels), :
                ] = product[:, i * LANES : (i + 1) * LANES]

    def store(q):
        at = pl.ds(q * part_slots, part_slots)
        return pltpu.make_async_copy(out.at[at], out_hbm.at[at], out_sem.at[q])

    for q in range(parts):

        def pick(j, q=q):
            slot = q * part_slots + j
            at = pl.ds(pl.multiple_of(table_ref[0, slot] * TROWS, TROWS), TROWS)
            out[slot] = crossed_rows[at, :].astype(jnp.bfloat16)

        loop(part_slots, pick, unroll=16)
        store(q).start()
    for q in range(parts):
        store(q).wait()


def ladder_kernel(size_ref, weight_ref, gen_ref, ham_ref, out_ref, gen, ham, wgen, wham, spread_weight):
    extent = gen_ref.shape[1]
    c = pl.program_id(0)
    size = size_ref[c]
    spread(weight_ref[0], spread_weight)

    def block(b):
        rows = pl.ds(pl.multiple_of(b * ROWS, ROWS), ROWS)
        inside = inside_of(b * ROWS, ROWS, extent, size)
        weight = jnp.tile(spread_weight[rows, :], (1, extent // LANES))
        g = jnp.where(inside, gen_ref[0, rows, :].astype(jnp.float32), 0.0)
        h = jnp.where(inside, ham_ref[0, rows, :].astype(jnp.float32), 0.0)
        gen[rows, :] = g.astype(jnp.bfloat16)
        ham[rows, :] = h.astype(jnp.bfloat16)
        wgen[rows, :] = (weight * g).astype(jnp.bfloat16)
        wham[rows, :] = (weight * h).astype(jnp.bfloat16)

    loop(extent // ROWS, block)
    wide = 2 * LANES
    for n in range(extent // wide):
        columns = slice(n * wide, (n + 1) * wide)
        first = jnp.dot(gen[...], wham[:, columns], preferred_element_type=jnp.float32)
        second = jnp.dot(ham[...], wgen[:, columns], preferred_element_type=jnp.float32)
        out_ref[0, :, columns] = ham[:, columns].astype(jnp.float32) + flow_step * (first - second)


def finish_kernel(size_ref, table_ref, base_hbm, in_hbm, out_hbm, base, arrived, rows_back, out, base_sem, in_sem, out_sem):
    channels, extent, _ = base.shape
    slots = arrived.shape[0]
    panels = extent // LANES
    parts, part_slots = chunks_of(slots, in_sem.shape[0])
    cuts, cut_rows = chunks_of(extent, 4)

    def load(q):
        at = pl.ds(q * part_slots, part_slots)
        return pltpu.make_async_copy(in_hbm.at[at], arrived.at[at], in_sem.at[q])

    def load_base(c):
        return pltpu.make_async_copy(base_hbm.at[c], base.at[c], base_sem.at[c])

    def store(c, k):
        at = pl.ds(k * cut_rows, cut_rows)
        return pltpu.make_async_copy(out.at[c, at], out_hbm.at[c, at], out_sem.at[c, k])

    for q in range(parts):
        load(q).start()
    for c in range(channels):
        load_base(c).start()
    for q in range(parts):
        load(q).wait()

        def place(j, q=q):
            slot = q * part_slots + j
            at = pl.ds(pl.multiple_of(table_ref[0, slot] * TROWS, TROWS), TROWS)
            rows_back[at, :] = arrived[slot].astype(jnp.float32)

        loop(part_slots, place, unroll=16)
    for c in range(channels):
        size = size_ref[c]
        load_base(c).wait()
        for k in range(cuts):

            def block(b, c=c, k=k, size=size):
                first = pl.multiple_of(k * cut_rows + b * ROWS, ROWS)
                rows = pl.ds(first, ROWS)
                start = (c * extent + first) * panels
                inside = inside_of(first, ROWS, extent, size)
                for p in range(panels):
                    lanes = slice(p * LANES, (p + 1) * LANES)
                    back = rows_back[pl.ds(start + p, ROWS, stride=panels), :]
                    total = base[c, rows, lanes] + flow_step * back
                    out[c, rows, lanes] = jnp.where(inside[:, lanes], total, 0.0)

            loop(cut_rows // ROWS, block, unroll=2)
            store(c, k).start()
    for c in range(channels):
        for k in range(cuts):
            store(c, k).wait()


ANY = functools.partial(pl.BlockSpec, memory_space=pl.ANY)
SMEM = functools.partial(pl.BlockSpec, memory_space=pltpu.SMEM)
WHOLE = functools.partial(pl.BlockSpec, memory_space=pltpu.VMEM)


def per_device(
    generator, hamiltonian, pair_weight, cross_weight, channel_size, send_table, receive_table
):
    channels, extent, _ = generator.shape
    slots = send_table.shape[1]
    tile_count = channels * extent * extent // (TILE * TILE)
    lane_rows = (tile_count + 1) * TROWS
    parts = 8
    devices = lax.axis_size(AXES)
    f32, bf16 = jnp.float32, jnp.bfloat16

    outgoing = pl.pallas_call(
        pack_kernel,
        out_shape=jax.ShapeDtypeStruct((slots, 2 * TROWS, LANES), bf16),
        in_specs=[SMEM(), SMEM(), ANY(), ANY()],
        out_specs=ANY(),
        scratch_shapes=[
            pltpu.VMEM((channels, extent, extent), bf16),
            pltpu.VMEM((channels, extent, extent), bf16),
            pltpu.VMEM((lane_rows, LANES), f32),
            pltpu.VMEM((lane_rows, LANES), f32),
            pltpu.VMEM((slots, 2 * TROWS, LANES), bf16),
            pltpu.SemaphoreType.DMA((2, 2 * channels)),
            pltpu.SemaphoreType.DMA((parts,)),
        ],
        compiler_params=params(),
        name="pack",
    )(channel_size, send_table, generator, hamiltonian)

    def exchange(tiles):
        swapped = lax.all_to_all(
            tiles.reshape(devices, slots // devices, *tiles.shape[1:]),
            AXES,
            split_axis=0,
            concat_axis=0,
            tiled=True,
        )
        return swapped.reshape(tiles.shape)

    arrived = exchange(outgoing)

    base = pl.pallas_call(
        ladder_kernel,
        grid=(channels,),
        out_shape=jax.ShapeDtypeStruct((channels, extent, extent), f32),
        in_specs=[
            SMEM(),
            pl.BlockSpec((1, 1, extent), lambda c: (c, 0, 0)),
            pl.BlockSpec((1, extent, extent), lambda c: (c, 0, 0)),
            pl.BlockSpec((1, extent, extent), lambda c: (c, 0, 0)),
        ],
        out_specs=pl.BlockSpec((1, extent, extent), lambda c: (c, 0, 0)),
        scratch_shapes=[pltpu.VMEM((extent, extent), bf16)] * 4
        + [pltpu.VMEM((extent, LANES), f32)],
        compiler_params=params(),
        name="ladder",
    )(channel_size, pair_weight[:, None, :], generator, hamiltonian)

    going_back = pl.pallas_call(
        cross_kernel,
        out_shape=jax.ShapeDtypeStruct((slots, TROWS, LANES), bf16),
        in_specs=[SMEM(), WHOLE(), ANY()],
        out_specs=ANY(),
        scratch_shapes=[
            pltpu.VMEM((slots, 2 * TROWS, LANES), bf16),
            pltpu.VMEM((lane_rows, LANES), f32),
            pltpu.VMEM((lane_rows, LANES), f32),
        ]
        + [pltpu.VMEM((extent, extent), bf16)] * 4
        + [
            pltpu.VMEM((channels, extent, LANES), f32),
            pltpu.VMEM((lane_rows, LANES), f32),
            pltpu.VMEM((slots, TROWS, LANES), bf16),
            pltpu.SemaphoreType.DMA((parts,)),
            pltpu.SemaphoreType.DMA((parts,)),
        ],
        compiler_params=params(),
        name="cross",
    )(receive_table, cross_weight, arrived)

    came_back = exchange(going_back)

    return pl.pallas_call(
        finish_kernel,
        out_shape=jax.ShapeDtypeStruct((channels, extent, extent), f32),
        in_specs=[SMEM(), SMEM(), ANY(), ANY()],
        out_specs=ANY(),
        scratch_shapes=[
            pltpu.VMEM((channels, extent, extent), f32),
            pltpu.VMEM((slots, TROWS, LANES), bf16),
            pltpu.VMEM((lane_rows, LANES), f32),
            pltpu.VMEM((channels, extent, extent), f32),
            pltpu.SemaphoreType.DMA((channels,)),
            pltpu.SemaphoreType.DMA((parts,)),
            pltpu.SemaphoreType.DMA((channels, 4)),
        ],
        compiler_params=params(),
        name="finish",
    )(channel_size, send_table, base, came_back)


def solution(mesh):
    in_specs = (
        P(AXES, None, None),
        P(AXES, None, None),
        P(AXES, None),
        P(AXES, None),
        P(AXES),
        P(AXES, None),
        P(AXES, None),
    )
    out_specs = P(AXES, None, None)
    return jax.shard_map(
        per_device, mesh=mesh, in_specs=in_specs, out_specs=out_specs, check_vma=False
    )
```

time: 267 us -> 174 us (0.65)
  local copies, waits for them, and re-layouts: 111 us -> 2.3 us
  blocking collectives: 0 us -> 92.6 us
  waiting for transfers between devices: 103 us -> 34.7 us
  Pallas kernels: 0 us -> 37.8 us
  matrix products: 21.3 us -> 0 us
  starting transfers between devices: 23.5 us -> 6.42 us
  other arithmetic: 5.93 us -> 0 us
    all_to_all x0 -> x1, blocking collectives: none -> 92.6 us  [exchange(): lax.all_to_all(tiles.reshape(devices, slots // devices, *tiles.shape[1:])...]
    all_to_all x3 -> x1, waiting for transfers between devices: 103 us -> 34.7 us  [exchange(): lax.all_to_all(tiles.reshape(devices, slots // devices, *tiles.shape[1:])...]
    pallas_call x0 -> x4, Pallas kernels: none -> 37.8 us  [the longest x1 14.2 us: per_device(): pl.pallas_call(cross_kernel, out_shape=jax.ShapeDtypeStruct((slots, TROWS...]
    gather x6 -> x0, local copies, waits for them, and re-layouts: 34.5 us -> none  [the longest x1 6.56 us: per_device(): masked_hamiltonian.reshape(tile_count, TILE * TILE)[send_pick]]
    all_to_all x6 -> x0, local copies, waits for them, and re-layouts: 30.1 us -> none  [the longest x2 10.1 us: per_device(): lax.all_to_all(outgoing_generator, ('group', 'chan'), split_axis=0, conca...]
    reshape x5 -> x0, local copies, waits for them, and re-layouts: 22.7 us -> none  [the longest x1 5.29 us: per_device(): arrived_hamiltonian[arrival_slot].reshape(channels, extent, extent)]
    dot_general x4 -> x0, matrix products: 21.3 us -> none  [the longest x2 11.8 us: commutator(): jnp.einsum('cij,cjk->cik', former, latter_weighted, preferred_element_typ...]
    scatter x2 -> x0, local copies, waits for them, and re-layouts: 18 us -> none  [inverse_of(): jnp.zeros((tile_count + 1,), jnp.int32).at[table_row].set(slots)]
  transfers between devices with their start and end apart: 3 -> 1, of which waited for: 3 -> 1; matrix products, arithmetic and copies ran while one was open for 17% -> 0% of each run, Pallas kernels for 0% -> 5%
where the time goes in v1:
time: 174 us
  blocking collectives  92.6 us (53%)
  Pallas kernels  37.8 us (22%)
  waiting for transfers between devices  34.7 us (20%)
  starting transfers between devices  6.42 us (4%)
  local copies, waits for them, and re-layouts  2.3 us (1%)
    all_to_all x1, blocking collectives, exchange(): lax.all_to_all(tiles.reshape(devices, slots // devices, *tiles.shape[1:])...  92.6 us
    all_to_all x1, waiting for transfers between devices, exchange(): lax.all_to_all(tiles.reshape(devices, slots // devices, *tiles.shape[1:])...  34.7 us
    pallas_call x1, Pallas kernels, per_device(): pl.pallas_call(cross_kernel, out_shape=jax.ShapeDtypeStruct((slots, TROWS...  14.2 us
    pallas_call x1, Pallas kernels, per_device(): pl.pallas_call(ladder_kernel, grid=(channels,), out_shape=jax.ShapeDtypeS...  9.27 us
    pallas_call x1, Pallas kernels, per_device(): pl.pallas_call(pack_kernel, out_shape=jax.ShapeDtypeStruct((slots, 2 * TR...  7.51 us
    pallas_call x1, Pallas kernels, per_device(): pl.pallas_call(finish_kernel, out_shape=jax.ShapeDtypeStruct((channels, e...  6.82 us
    all_to_all x1, starting transfers between devices, exchange(): lax.all_to_all(tiles.reshape(devices, slots // devices, *tiles.shape[1:])...  6.42 us
  transfers between devices with their start and end apart: 1, of which 1 were waited for; matrix products, arithmetic and copies ran while one was open for 0% of the time, Pallas kernels for 5%

profile of v1, /device:TPU:1, one launch (start us, length us, event | category | flops | bytes accessed | tf_op | source)
XLA Modules:
  0.0 173.9 jit_solution(17976293822190185787)
XLA Ops:
  0.0 7.5 %pack.1 = bf16[1664,16,128]{2,1,0:T(8,128)(2,1)} custom-call(s32[2]{0:T(128)} %size_ref.5, s32[1,1664]{1,0:T(1,128)} %table_ref.5, bf16[2,768,768]{2,1,0:T(8,128)(2,1)} %gen_hbm.1, bf16[2,768,768]{2,1,0:T(8,128)(2,1)} %ham_hbm.1), custom_call_target="tpu_custom_call" | custom-call | tf_op jit(solution)/shard_map/pack/pallas_call | solution.py:275
  7.5 92.6 %all_to_all.10 = bf16[128,13,16,128]{3,2,1,0:T(8,128)(2,1)} all-to-all(bf16[128,13,16,128]{3,2,1,0:T(8,128)(2,1)} %bitcast.4), channel_id=1, replica_groups=mesh['group'=4,'chan'=32] {'group','chan'}, dimensions={0} | all-to-all | bytes 13631488 | tf_op jit(solution)/shard_map/all_to_all | solution.py:294
  100.1 14.2 %cross.1 = bf16[1664,8,128]{2,1,0:T(8,128)(2,1)} custom-call(s32[1,1664]{1,0:T(1,128)} %table_ref.4, f32[2,768]{1,0:T(2,128)} %weight_ref.1, bf16[1664,16,128]{2,1,0:T(8,128)(2,1)} %bitcast.5), custom_call_target="tpu_custom_call" | custom-call | tf_op jit(solution)/shard_map/cross/pallas_call | solution.py:322
  114.3 0.0 copy-start.1
  114.3 6.4 %all-to-all-start.1 = ((bf16[128,13,8,128]{3,2,1,0:T(8,128)(2,1)}), bf16[128,13,8,128]{3,2,1,0:T(8,128)(2,1)S(1)}, u32[]{:S(2)}, u32[]{:S(2)}) async-start(bf16[128,13,8,128]{3,2,1,0:T(8,128)(2,1)} %bitcast.6), calls=%async_computation.1 | async-start | bytes 6815744 | tf_op jit(solution)/shard_map/all_to_all | solution.py:294
  120.8 0.0 copy-done.1
  120.8 0.6 broadcast_in_dim.3.weight_ref
  121.4 9.3 %ladder.1.base_hbm = f32[2,768,768]{2,1,0:T(8,128)} custom-call(s32[2]{0:T(128)} %size_ref.5, f32[2,1,768]{2,1,0:T(1,128)} %broadcast_in_dim.3.weight_ref, bf16[2,768,768]{2,1,0:T(8,128)(2,1)} %gen_hbm.1, bf16[2,768,768]{2,1,0:T(8,128)(2,1)} %ham_hbm.1), custom_call_target="tpu_custom_call" | custom-call | tf_op jit(solution)/shard_map/ladder/pallas_call | solution.py:305
  130.6 34.7 %all-to-all-done.1 = bf16[128,13,8,128]{3,2,1,0:T(8,128)(2,1)S(1)} async-done(((bf16[128,13,8,128]{3,2,1,0:T(8,128)(2,1)}), bf16[128,13,8,128]{3,2,1,0:T(8,128)(2,1)S(1)}, u32[]{:S(2)}, u32[]{:S(2)}) %all-to-all-start.1) | async-done | bytes 3407904 | tf_op jit(solution)/shard_map/all_to_all | solution.py:294
  165.3 0.0 copy-start
  165.3 1.7 copy-done
  167.0 6.8 %finish.1 = f32[2,768,768]{2,1,0:T(8,128)} custom-call(s32[2]{0:T(128)} %size_ref.5, s32[1,1664]{1,0:T(1,128)} %table_ref.5, f32[2,768,768]{2,1,0:T(8,128)} %ladder.1.base_hbm, bf16[1664,8,128]{2,1,0:T(8,128)(2,1)} %bitcast.7), custom_call_target="tpu_custom_call" | custom-call | tf_op jit(solution)/shard_map/finish/pallas_call | solution.py:346
Async XLA Ops:
  114.3 6.4 %copy-start.1 = (f32[2,768]{1,0:T(2,128)S(1)}, f32[2,768]{1,0:T(2,128)}, u32[]{:S(2)}) copy-start(f32[2,768]{1,0:T(2,128)} %param.9) | copy-start | bytes 18436
  114.3 51.0 %all-to-all-start.1 = ((bf16[128,13,8,128]{3,2,1,0:T(8,128)(2,1)}), bf16[128,13,8,128]{3,2,1,0:T(8,128)(2,1)S(1)}, u32[]{:S(2)}, u32[]{:S(2)}) async-start(bf16[128,13,8,128]{3,2,1,0:T(8,128)(2,1)} %bitcast.6), calls=%async_computation.1 | async-start | bytes 6815744 | tf_op jit(solution)/shard_map/all_to_all | solution.py:294
  165.3 1.7 copy-start

commit v2 on v1

v2 whole, which is shorter than its diff:
```python
import functools

import jax
import jax.numpy as jnp
from jax import lax
from jax.experimental import pallas as pl
from jax.experimental.pallas import tpu as pltpu
from jax.sharding import PartitionSpec as P

TILE = 32
LANES = 128
TROWS = TILE * TILE // LANES
ROWS = 16
SLOTS = 16
PAIRS_A_TURN = 13
HALF_WORD = 16

flow_step = 0.5

AXES = ("group", "chan")


def params(mebibytes):
    return pltpu.CompilerParams(vmem_limit_bytes=mebibytes * 1024 * 1024)


def chunks_of(total, count):
    while total % count:
        count -= 1
    return count, total // count


def loop(count, body, unroll=1):
    lax.fori_loop(0, count, lambda i, _: (body(i), 0)[1], 0, unroll=unroll)


def inside_of(first_row, rows, columns, size):
    row = lax.broadcasted_iota(jnp.int32, (rows, columns), 0) + first_row
    column = lax.broadcasted_iota(jnp.int32, (rows, columns), 1)
    return (row < size) & (column < size)


def spread(weight_row, out_ref):
    extent = weight_row.shape[1]
    for k in range(extent // LANES):
        piece = weight_row[:, k * LANES : (k + 1) * LANES]
        out_ref[k * LANES : (k + 1) * LANES, :] = jnp.transpose(
            jnp.broadcast_to(piece, (LANES, LANES))
        )


def pack_kernel(size_hbm, table_hbm, gen_hbm, ham_hbm, out_hbm, size_ref, table_ref, gen, ham, rows, out, small_sem, in_sem, out_sem):
    channels, extent, _ = gen.shape
    slots = out.shape[0]
    panels = extent // LANES
    half = rows.shape[0] // 2
    parts, part_rows = chunks_of(extent, 2)
    out_parts = out_sem.shape[0]
    out_slots = slots // out_parts

    sizes = pltpu.make_async_copy(size_hbm, size_ref, small_sem.at[0])
    table = pltpu.make_async_copy(table_hbm, table_ref, small_sem.at[1])
    sizes.start()

    def loads(c, h):
        at = pl.ds(h * part_rows, part_rows)
        k = c * parts + h
        return (
            pltpu.make_async_copy(gen_hbm.at[c, at], gen.at[c, at], in_sem.at[0, k]),
            pltpu.make_async_copy(ham_hbm.at[c, at], ham.at[c, at], in_sem.at[1, k]),
        )

    for c in range(channels):
        for h in range(parts):
            for copy in loads(c, h):
                copy.start()
    table.start()
    sizes.wait()
    for c in range(channels):
        size = size_ref[c]
        for h in range(parts):
            for copy in loads(c, h):
                copy.wait()

            def block(b, c=c, h=h, size=size):
                first = pl.multiple_of(h * part_rows + b * ROWS, ROWS)
                inside = inside_of(first, ROWS, extent, size)
                base = (c * extent + first) * panels
                for source, offset in ((gen, 0), (ham, half)):
                    values = source[c, pl.ds(first, ROWS), :].astype(jnp.float32)
                    values = jnp.where(inside, values, 0.0)
                    for p in range(panels):
                        rows[pl.ds(base + (offset + p), ROWS, stride=panels), :] = values[
                            :, p * LANES : (p + 1) * LANES
                        ]

            loop(part_rows // ROWS, block, unroll=2)
    table.wait()

    def store(q):
        at = pl.ds(q * out_slots, out_slots)
        return pltpu.make_async_copy(out.at[at], out_hbm.at[at], out_sem.at[q])

    for q in range(out_parts):

        def pick(i, q=q):
            first_slot = q * out_slots + i * SLOTS
            for u in range(SLOTS):
                first = pl.multiple_of(table_ref[0, first_slot + u] * TROWS, TROWS)
                g = rows[pl.ds(first, TROWS), :]
                h = rows[pl.ds(first + half, TROWS), :]
                out[first_slot + u] = jnp.concatenate([g, h], axis=0).astype(jnp.bfloat16)

        loop(out_slots // SLOTS, pick)
        store(q).start()
    for q in range(out_parts):
        store(q).wait()


def rows_kernel(send_ref, receive_ref, send_rows, receive_rows):
    pairs = send_rows.shape[1]

    def one(i):
        for table, packed in ((send_ref, send_rows), (receive_ref, receive_rows)):
            low = table[0, i] * TROWS
            packed[0, i] = low + table[0, i + pairs] * (TROWS << HALF_WORD)

    loop(pairs, one, unroll=8)


def each_slot(packed, start, count, body):
    pairs = packed.shape[1]

    def several(i):
        for u in range(PAIRS_A_TURN):
            slot = start + i * PAIRS_A_TURN + u
            word = packed[0, slot]
            low = pl.multiple_of(word & ((1 << HALF_WORD) - 1), TROWS)
            high = pl.multiple_of(lax.shift_right_logical(word, HALF_WORD), TROWS)
            body(slot, low)
            body(slot + pairs, high)

    loop(count // PAIRS_A_TURN, several)


def paired_copies(source, target, sem, q):
    half = source.shape[0] // 2
    part = half // sem.shape[1]
    copies = []
    for k in range(2):
        at = pl.ds(k * half + q * part, part)
        copies.append(pltpu.make_async_copy(source.at[at], target.at[at], sem.at[k, q]))
    return copies


def cross_kernel(packed, weight_ref, in_hbm, out_hbm, arrived, both_rows, gen, ham, wgen, wham, spread_weight, crossed_rows, out, in_sem, out_sem):
    channels, extent = weight_ref.shape
    panels = extent // LANES
    other = both_rows.shape[0] // 2
    parts = in_sem.shape[1]
    part_pairs = packed.shape[1] // parts

    def place(slot, row):
        both = arrived[slot].astype(jnp.float32)
        both_rows[pl.ds(row, TROWS), :] = both[:TROWS]
        both_rows[pl.ds(row + other, TROWS), :] = both[TROWS:]

    def give(slot, row):
        out[slot] = crossed_rows[pl.ds(row, TROWS), :].astype(jnp.bfloat16)

    for q in range(parts):
        for copy in paired_copies(in_hbm, arrived, in_sem, q):
            copy.start()
    for c in range(channels):
        spread(weight_ref[c : c + 1, :], spread_weight.at[c])
    for q in range(parts):
        for copy in paired_copies(in_hbm, arrived, in_sem, q):
            copy.wait()
        each_slot(packed, q * part_pairs, part_pairs, place)
    for c in range(channels):

        def block(b, c=c):
            first = pl.multiple_of(b * ROWS, ROWS)
            rows = pl.ds(first, ROWS)
            base = (c * extent + first) * panels
            weight = spread_weight[c, rows, :]
            for p in range(0, panels, 2):
                lanes = slice(p * LANES, (p + 2) * LANES)
                g = [both_rows[pl.ds(base + (p + i), ROWS, stride=panels), :] for i in range(2)]
                h = [
                    both_rows[pl.ds(base + (other + p + i), ROWS, stride=panels), :]
                    for i in range(2)
                ]
                for target, pair in (
                    (gen, g),
                    (ham, h),
                    (wgen, [weight * x for x in g]),
                    (wham, [weight * x for x in h]),
                ):
                    target[rows, lanes] = jnp.concatenate(pair, axis=1).astype(jnp.bfloat16)

        loop(extent // ROWS, block, unroll=2)
        step = 2 * LANES
        for n in range(extent // step):
            columns = slice(n * step, (n + 1) * step)
            first = jnp.dot(gen[...], wham[:, columns], preferred_element_type=jnp.float32)
            second = jnp.dot(ham[...], wgen[:, columns], preferred_element_type=jnp.float32)
            product = first - second
            for i in range(step // LANES):
                p = n * (step // LANES) + i
                crossed_rows[
                    pl.ds(c * extent * panels + p, extent, stride=panels), :
                ] = product[:, i * LANES : (i + 1) * LANES]

    for q in range(parts):
        each_slot(packed, q * part_pairs, part_pairs, give)
        for copy in paired_copies(out, out_hbm, out_sem, q):
            copy.start()
    for q in range(parts):
        for copy in paired_copies(out, out_hbm, out_sem, q):
            copy.wait()


def ladder_kernel(size_ref, weight_ref, gen_ref, ham_ref, out_ref, gen, ham, wgen, wham, spread_weight):
    channels, extent, _ = gen_ref.shape
    for c in range(channels):
        size = size_ref[c]
        spread(weight_ref[c : c + 1, :], spread_weight)

        def block(b, c=c, size=size):
            rows = pl.ds(pl.multiple_of(b * ROWS, ROWS), ROWS)
            inside = inside_of(b * ROWS, ROWS, extent, size)
            weight = jnp.tile(spread_weight[rows, :], (1, extent // LANES))
            g = jnp.where(inside, gen_ref[c, rows, :].astype(jnp.float32), 0.0)
            h = jnp.where(inside, ham_ref[c, rows, :].astype(jnp.float32), 0.0)
            gen[rows, :] = g.astype(jnp.bfloat16)
            ham[rows, :] = h.astype(jnp.bfloat16)
            wgen[rows, :] = (weight * g).astype(jnp.bfloat16)
            wham[rows, :] = (weight * h).astype(jnp.bfloat16)

        loop(extent // ROWS, block)
        step = 2 * LANES
        for n in range(extent // step):
            columns = slice(n * step, (n + 1) * step)
            first = jnp.dot(gen[...], wham[:, columns], preferred_element_type=jnp.float32)
            second = jnp.dot(ham[...], wgen[:, columns], preferred_element_type=jnp.float32)
            out_ref[c, :, columns] = ham[:, columns].astype(jnp.float32) + flow_step * (
                first - second
            )


def finish_kernel(size_ref, packed, base_hbm, in_hbm, out_hbm, base, arrived, back_rows, out, base_sem, in_sem, out_sem):
    channels, extent, _ = base.shape
    panels = extent // LANES
    parts = in_sem.shape[1]
    part_pairs = packed.shape[1] // parts
    cuts = out_sem.shape[1]
    cut_rows = extent // cuts

    def load_base(c):
        return pltpu.make_async_copy(base_hbm.at[c], base.at[c], base_sem.at[c])

    def store(c, k):
        at = pl.ds(k * cut_rows, cut_rows)
        return pltpu.make_async_copy(out.at[c, at], out_hbm.at[c, at], out_sem.at[c, k])

    def place(slot, row):
        back_rows[pl.ds(row, TROWS), :] = arrived[slot].astype(jnp.float32)

    for q in range(parts):
        for copy in paired_copies(in_hbm, arrived, in_sem, q):
            copy.start()
    for c in range(channels):
        load_base(c).start()
    for q in range(parts):
        for copy in paired_copies(in_hbm, arrived, in_sem, q):
            copy.wait()
        each_slot(packed, q * part_pairs, part_pairs, place)
    for c in range(channels):
        size = size_ref[c]
        load_base(c).wait()
        for k in range(cuts):

            def block(b, c=c, k=k, size=size):
                first = pl.multiple_of(k * cut_rows + b * ROWS, ROWS)
                rows = pl.ds(first, ROWS)
                start = (c * extent + first) * panels
                inside = inside_of(first, ROWS, extent, size)
                for p in range(panels):
                    lanes = slice(p * LANES, (p + 1) * LANES)
                    back = back_rows[pl.ds(start + p, ROWS, stride=panels), :]
                    total = base[c, rows, lanes] + flow_step * back
                    out[c, rows, lanes] = jnp.where(inside[:, lanes], total, 0.0)

            loop(cut_rows // ROWS, block, unroll=2)
            store(c, k).start()
    for c in range(channels):
        for k in range(cuts):
            store(c, k).wait()


HBM = functools.partial(pl.BlockSpec, memory_space=pltpu.HBM)
SMEM = functools.partial(pl.BlockSpec, memory_space=pltpu.SMEM)
WHOLE = functools.partial(pl.BlockSpec, memory_space=pltpu.VMEM)


def per_device(
    generator, hamiltonian, pair_weight, cross_weight, channel_size, send_table, receive_table
):
    channels, extent, _ = generator.shape
    slots = send_table.shape[1]
    panels = extent // LANES
    lane_rows = channels * extent * panels + TROWS
    parts = 8
    devices = lax.axis_size(AXES)
    f32, bf16 = jnp.float32, jnp.bfloat16

    outgoing = pl.pallas_call(
        pack_kernel,
        out_shape=jax.ShapeDtypeStruct((slots, 2 * TROWS, LANES), bf16),
        in_specs=[HBM()] * 4,
        out_specs=HBM(),
        scratch_shapes=[
            pltpu.SMEM(channel_size.shape, jnp.int32),
            pltpu.SMEM(send_table.shape, jnp.int32),
            pltpu.VMEM((channels, extent, extent), bf16),
            pltpu.VMEM((channels, extent, extent), bf16),
            pltpu.VMEM((2 * lane_rows, LANES), f32),
            pltpu.VMEM((slots, 2 * TROWS, LANES), bf16),
            pltpu.SemaphoreType.DMA((2,)),
            pltpu.SemaphoreType.DMA((2, 2 * channels)),
            pltpu.SemaphoreType.DMA((parts,)),
        ],
        compiler_params=params(60),
        name="pack",
    )(channel_size, send_table, generator, hamiltonian)

    def exchange(tiles):
        swapped = lax.all_to_all(
            tiles.reshape(devices, slots // devices, *tiles.shape[1:]),
            AXES,
            split_axis=0,
            concat_axis=0,
            tiled=True,
        )
        return swapped.reshape(tiles.shape)

    arrived = exchange(outgoing)

    send_rows, receive_rows = pl.pallas_call(
        rows_kernel,
        out_shape=[jax.ShapeDtypeStruct((1, slots // 2), jnp.int32)] * 2,
        in_specs=[SMEM(), SMEM()],
        out_specs=[SMEM(), SMEM()],
        compiler_params=params(2),
        name="rows",
    )(send_table, receive_table)

    base = pl.pallas_call(
        ladder_kernel,
        out_shape=jax.ShapeDtypeStruct((channels, extent, extent), f32),
        in_specs=[SMEM(), WHOLE(), WHOLE(), WHOLE()],
        out_specs=WHOLE(),
        scratch_shapes=[pltpu.VMEM((extent, extent), bf16)] * 4
        + [pltpu.VMEM((extent, LANES), f32)],
        compiler_params=params(20),
        name="ladder",
    )(channel_size, pair_weight, generator, hamiltonian)

    going_back = pl.pallas_call(
        cross_kernel,
        out_shape=jax.ShapeDtypeStruct((slots, TROWS, LANES), bf16),
        in_specs=[SMEM(), WHOLE(), HBM()],
        out_specs=HBM(),
        scratch_shapes=[
            pltpu.VMEM((slots, 2 * TROWS, LANES), bf16),
            pltpu.VMEM((2 * lane_rows, LANES), f32),
        ]
        + [pltpu.VMEM((extent, extent), bf16)] * 4
        + [
            pltpu.VMEM((channels, extent, LANES), f32),
            pltpu.VMEM((lane_rows, LANES), f32),
            pltpu.VMEM((slots, TROWS, LANES), bf16),
            pltpu.SemaphoreType.DMA((2, parts)),
            pltpu.SemaphoreType.DMA((2, parts)),
        ],
        compiler_params=params(60),
        name="cross",
    )(receive_rows, cross_weight, arrived)

    came_back = exchange(going_back)

    return pl.pallas_call(
        finish_kernel,
        out_shape=jax.ShapeDtypeStruct((channels, extent, extent), f32),
        in_specs=[SMEM(), SMEM(), HBM(), HBM()],
        out_specs=HBM(),
        scratch_shapes=[
            pltpu.VMEM((channels, extent, extent), f32),
            pltpu.VMEM((slots, TROWS, LANES), bf16),
            pltpu.VMEM((lane_rows, LANES), f32),
            pltpu.VMEM((channels, extent, extent), f32),
            pltpu.SemaphoreType.DMA((channels,)),
            pltpu.SemaphoreType.DMA((2, parts)),
            pltpu.SemaphoreType.DMA((channels, 4)),
        ],
        compiler_params=params(60),
        name="finish",
    )(channel_size, send_rows, base, came_back)


def solution(mesh):
    in_specs = (
        P(AXES, None, None),
        P(AXES, None, None),
        P(AXES, None),
        P(AXES, None),
        P(AXES),
        P(AXES, None),
        P(AXES, None),
    )
    out_specs = P(AXES, None, None)
    return jax.shard_map(
        per_device, mesh=mesh, in_specs=in_specs, out_specs=out_specs, check_vma=False
    )
```

time: 174 us -> 171 us (0.983)
  blocking collectives: 92.6 us -> 0 us
  waiting for transfers between devices: 34.7 us -> 108 us
  starting transfers between devices: 6.42 us -> 21.4 us
  local copies, waits for them, and re-layouts: 2.3 us -> 4.99 us
  Pallas kernels: 37.8 us -> 35.9 us
    all_to_all x1 -> x0, blocking collectives: 92.6 us -> none  [exchange(): lax.all_to_all(tiles.reshape(devices, slots // devices, *tiles.shape[1:])...]
    all_to_all x1 -> x2, waiting for transfers between devices: 34.7 us -> 108 us  [exchange(): lax.all_to_all(tiles.reshape(devices, slots // devices, *tiles.shape[1:])...]
    all_to_all x1 -> x2, starting transfers between devices: 6.42 us -> 21.4 us  [exchange(): lax.all_to_all(tiles.reshape(devices, slots // devices, *tiles.shape[1:])...]
    unnamed x4 -> x18, local copies, waits for them, and re-layouts: 1.71 us -> 4.99 us
    pallas_call x1 -> x2, Pallas kernels: 9.27 us -> 12 us  [the longest x1 6.49 us: per_device(): pl.pallas_call(ladder_kernel, out_shape=jax.ShapeDtypeStruct((channels, e...]
    pallas_call x1, Pallas kernels: 14.2 us -> 11.6 us  [per_device(): pl.pallas_call(cross_kernel, out_shape=jax.ShapeDtypeStruct((slots, TROWS...]
  transfers between devices with their start and end apart: 1 -> 2, of which waited for: 1 -> 2; matrix products, arithmetic and copies ran while one was open for 0% -> 0% of each run, Pallas kernels for 5% -> 7%
where the time goes in v2:
time: 171 us
  waiting for transfers between devices  108 us (63%)
  Pallas kernels  35.9 us (21%)
  starting transfers between devices  21.4 us (13%)
  local copies, waits for them, and re-layouts  4.99 us (3%)
    all_to_all x2, waiting for transfers between devices, exchange(): lax.all_to_all(tiles.reshape(devices, slots // devices, *tiles.shape[1:])...  108 us
    all_to_all x2, starting transfers between devices, exchange(): lax.all_to_all(tiles.reshape(devices, slots // devices, *tiles.shape[1:])...  21.4 us
    pallas_call x1, Pallas kernels, per_device(): pl.pallas_call(cross_kernel, out_shape=jax.ShapeDtypeStruct((slots, TROWS...  11.6 us
    pallas_call x1, Pallas kernels, per_device(): pl.pallas_call(ladder_kernel, out_shape=jax.ShapeDtypeStruct((channels, e...  6.49 us
    pallas_call x1, Pallas kernels, per_device(): pl.pallas_call(finish_kernel, out_shape=jax.ShapeDtypeStruct((channels, e...  6.17 us
    pallas_call x1, Pallas kernels, per_device(): pl.pallas_call(pack_kernel, out_shape=jax.ShapeDtypeStruct((slots, 2 * TR...  6.11 us
    pallas_call x1, Pallas kernels, per_device(): pl.pallas_call(rows_kernel, out_shape=[jax.ShapeDtypeStruct((1, slots //...  5.5 us
    unnamed x18, local copies, waits for them, and re-layouts  4.99 us
  transfers between devices with their start and end apart: 2, of which 2 were waited for; matrix products, arithmetic and copies ran while one was open for 0% of the time, Pallas kernels for 7%

profile of v2, /device:TPU:1, one launch (start us, length us, event | category | flops | bytes accessed | tf_op | source)
XLA Modules:
  0.0 170.9 jit_solution(106872776983230726)
XLA Ops:
  0.0 6.1 %pack.1 = bf16[1664,16,128]{2,1,0:T(8,128)(2,1)} custom-call(s32[2]{0:T(128)} %size_ref.3, s32[1,1664]{1,0:T(1,128)} %table_hbm.1, bf16[2,768,768]{2,1,0:T(8,128)(2,1)} %gen_hbm.1, bf16[2,768,768]{2,1,0:T(8,128)(2,1)} %ham_hbm.1), custom_call_target="tpu_custom_call" | custom-call | tf_op jit(solution)/shard_map/pack/pallas_call | solution.py:318
  6.1 0.0 copy-start.3
  6.1 0.0 copy-start.4
  6.1 11.9 %all-to-all-start = ((bf16[128,13,16,128]{3,2,1,0:T(8,128)(2,1)}), bf16[128,13,16,128]{3,2,1,0:T(8,128)(2,1)}, u32[]{:S(2)}, u32[]{:S(2)}) async-start(bf16[128,13,16,128]{3,2,1,0:T(8,128)(2,1)} %bitcast.4), calls=%async_computation | async-start | bytes 13631488 | tf_op jit(solution)/shard_map/all_to_all | solution.py:339
  18.0 0.0 copy-done.3
  18.1 0.0 copy-done.4
  18.1 5.5 %rows.1 = (s32[1,832]{1,0:T(1,128)S(1)}, s32[1,832]{1,0:T(1,128)S(1)}) custom-call(s32[1,1664]{1,0:T(1,128)S(1)} %copy-done.3, s32[1,1664]{1,0:T(1,128)S(1)} %copy-done.4), custom_call_target="tpu_custom_call" | custom-call | tf_op jit(solution)/shard_map/rows/pallas_call | solution.py:350
  23.6 0.0 copy-start.7
  23.6 0.6 copy-done.7
  24.2 0.0 copy-start.8
  24.2 0.6 copy-done.8
  24.8 74.5 %all-to-all-done = bf16[128,13,16,128]{3,2,1,0:T(8,128)(2,1)} async-done(((bf16[128,13,16,128]{3,2,1,0:T(8,128)(2,1)}), bf16[128,13,16,128]{3,2,1,0:T(8,128)(2,1)}, u32[]{:S(2)}, u32[]{:S(2)}) %all-to-all-start) | async-done | bytes 6815776 | tf_op jit(solution)/shard_map/all_to_all | solution.py:339
  99.3 11.6 %cross.1 = bf16[1664,8,128]{2,1,0:T(8,128)(2,1)} custom-call(s32[1,832]{1,0:T(1,128)} %copy-done.7, f32[2,768]{1,0:T(2,128)} %weight_ref.3, bf16[1664,16,128]{2,1,0:T(8,128)(2,1)} %bitcast.1.in_hbm), custom_call_target="tpu_custom_call" | custom-call | tf_op jit(solution)/shard_map/cross/pallas_call | solution.py:370
  110.9 0.0 copy-start.1
  110.9 0.0 copy-start.5
  110.9 0.0 copy-start.6
  110.9 9.5 %all-to-all-start.1 = ((bf16[128,13,8,128]{3,2,1,0:T(8,128)(2,1)}), bf16[128,13,8,128]{3,2,1,0:T(8,128)(2,1)}, u32[]{:S(2)}, u32[]{:S(2)}) async-start(bf16[128,13,8,128]{3,2,1,0:T(8,128)(2,1)} %bitcast.5), calls=%async_computation.1 | async-start | bytes 6815744 | tf_op jit(solution)/shard_map/all_to_all | solution.py:339
  120.5 0.0 copy-done.1
  120.5 0.0 copy-done.5
  120.5 0.0 copy-done.6
  120.5 0.0 copy-start.2
  120.5 1.7 copy-done.2
  122.2 6.5 %ladder.1.base_hbm = f32[2,768,768]{2,1,0:T(8,128)S(1)} custom-call(s32[2]{0:T(128)S(1)} %copy-done.6, f32[2,768]{1,0:T(2,128)S(1)} %copy-done.5, bf16[2,768,768]{2,1,0:T(8,128)(2,1)S(1)} %copy-done.1, bf16[2,768,768]{2,1,0:T(8,128)(2,1)S(1)} %copy-done.2), custom_call_target="tpu_custom_call" | custom-call | tf_op jit(solution)/shard_map/ladder/pallas_call | solution.py:359
  128.7 0.0 copy-start
  128.7 2.1 %copy-done = f32[2,768,768]{2,1,0:T(8,128)} copy-done((f32[2,768,768]{2,1,0:T(8,128)}, f32[2,768,768]{2,1,0:T(8,128)S(1)}, u32[]{:S(2)}) %copy-start) | copy-done | bytes 4718616
  130.8 34.0 %all-to-all-done.1 = bf16[128,13,8,128]{3,2,1,0:T(8,128)(2,1)} async-done(((bf16[128,13,8,128]{3,2,1,0:T(8,128)(2,1)}), bf16[128,13,8,128]{3,2,1,0:T(8,128)(2,1)}, u32[]{:S(2)}, u32[]{:S(2)}) %all-to-all-start.1) | async-done | bytes 3407904 | tf_op jit(solution)/shard_map/all_to_all | solution.py:339
  164.8 6.2 %finish.1 = f32[2,768,768]{2,1,0:T(8,128)} custom-call(s32[2]{0:T(128)} %size_ref.3, s32[1,832]{1,0:T(1,128)} %copy-done.8, f32[2,768,768]{2,1,0:T(8,128)} %copy-done, bf16[1664,8,128]{2,1,0:T(8,128)(2,1)} %bitcast.3.in_hbm), custom_call_target="tpu_custom_call" | custom-call | tf_op jit(solution)/shard_map/finish/pallas_call | solution.py:393
Async XLA Ops:
  6.1 11.9 %copy-start.3 = (s32[1,1664]{1,0:T(1,128)S(1)}, s32[1,1664]{1,0:T(1,128)}, u32[]{:S(2)}) copy-start(s32[1,1664]{1,0:T(1,128)} %table_hbm.1) | copy-start | bytes 19972
  6.1 11.9 %copy-start.4 = (s32[1,1664]{1,0:T(1,128)S(1)}, s32[1,1664]{1,0:T(1,128)}, u32[]{:S(2)}) copy-start(s32[1,1664]{1,0:T(1,128)} %receive_ref.1) | copy-start | bytes 19972
  6.1 93.1 %all-to-all-start = ((bf16[128,13,16,128]{3,2,1,0:T(8,128)(2,1)}), bf16[128,13,16,128]{3,2,1,0:T(8,128)(2,1)}, u32[]{:S(2)}, u32[]{:S(2)}) async-start(bf16[128,13,16,128]{3,2,1,0:T(8,128)(2,1)} %bitcast.4), calls=%async_computation | async-start | bytes 13631488 | tf_op jit(solution)/shard_map/all_to_all | solution.py:339
  23.6 0.6 copy-start.7
  24.2 0.6 copy-start.8
  110.9 9.6 %copy-start.1 = (bf16[2,768,768]{2,1,0:T(8,128)(2,1)S(1)}, bf16[2,768,768]{2,1,0:T(8,128)(2,1)}, u32[]{:S(2)}) copy-start(bf16[2,768,768]{2,1,0:T(8,128)(2,1)} %gen_hbm.1) | copy-start | bytes 7077892
  110.9 9.6 %copy-start.5 = (f32[2,768]{1,0:T(2,128)S(1)}, f32[2,768]{1,0:T(2,128)}, u32[]{:S(2)}) copy-start(f32[2,768]{1,0:T(2,128)} %weight_ref.2) | copy-start | bytes 18436
  110.9 9.6 %copy-start.6 = (s32[2]{0:T(128)S(1)}, s32[2]{0:T(128)}, u32[]{:S(2)}) copy-start(s32[2]{0:T(128)} %size_ref.3) | copy-start | bytes 28
  110.9 53.8 %all-to-all-start.1 = ((bf16[128,13,8,128]{3,2,1,0:T(8,128)(2,1)}), bf16[128,13,8,128]{3,2,1,0:T(8,128)(2,1)}, u32[]{:S(2)}, u32[]{:S(2)}) async-start(bf16[128,13,8,128]{3,2,1,0:T(8,128)(2,1)} %bitcast.5), calls=%async_computation.1 | async-start | bytes 6815744 | tf_op jit(solution)/shard_map/all_to_all | solution.py:339
  120.5 1.7 copy-start.2
  128.7 2.1 %copy-start = (f32[2,768,768]{2,1,0:T(8,128)}, f32[2,768,768]{2,1,0:T(8,128)S(1)}, u32[]{:S(2)}) copy-start(f32[2,768,768]{2,1,0:T(8,128)S(1)} %ladder.1.base_hbm) | copy-start | bytes 14155780

commit v3 on v2

--- a/solution.py
+++ b/solution.py
@@ -11,13 +11,27 @@
 LANES = 128
 TROWS = TILE * TILE // LANES
 ROWS = 16
-SLOTS = 16
-PAIRS_A_TURN = 13
-HALF_WORD = 16
 
 flow_step = 0.5
 
+PACK_MIB, LADDER_MIB, CROSS_MIB, FINISH_MIB = 60, 20, 40, 50
+
 AXES = ("group", "chan")
+X_BITS, Y_BITS, Z_BITS, CORE_BITS = 2, 2, 2, 1
+DEVICES = 1 << (X_BITS + Y_BITS + Z_BITS + CORE_BITS)
+
+
+def device_at(place):
+    x = place & ((1 << X_BITS) - 1)
+    place = place >> X_BITS
+    z = place & ((1 << Z_BITS) - 1)
+    place = place >> Z_BITS
+    core = place & ((1 << CORE_BITS) - 1)
+    y = place >> CORE_BITS
+    return (((((x << Y_BITS) | y) << Z_BITS) | z) << CORE_BITS) | core
+
+
+ORDER = [device_at(place) for place in range(DEVICES)]
 
 
 def params(mebibytes):
@@ -49,18 +63,20 @@
         )
 
 
-def pack_kernel(size_hbm, table_hbm, gen_hbm, ham_hbm, out_hbm, size_ref, table_ref, gen, ham, rows, out, small_sem, in_sem, out_sem):
+def pack_kernel(size_hbm, table_hbm, gen_hbm, ham_hbm, out_hbm, size_ref, table, words, first_rows, gen, ham, rows, out, small_sem, in_sem, out_sem):
     channels, extent, _ = gen.shape
-    slots = out.shape[0]
     panels = extent // LANES
     half = rows.shape[0] // 2
     parts, part_rows = chunks_of(extent, 2)
+    capacity = first_rows.shape[1] // DEVICES
     out_parts = out_sem.shape[0]
-    out_slots = slots // out_parts
-
-    sizes = pltpu.make_async_copy(size_hbm, size_ref, small_sem.at[0])
-    table = pltpu.make_async_copy(table_hbm, table_ref, small_sem.at[1])
-    sizes.start()
+    out_places = DEVICES // out_parts
+
+    read_table = pltpu.make_async_copy(table_hbm, table, small_sem.at[0])
+    read_sizes = pltpu.make_async_copy(size_hbm, size_ref, small_sem.at[1])
+    give_rows = pltpu.make_async_copy(words, first_rows, small_sem.at[2])
+    read_table.start()
+    read_sizes.start()
 
     def loads(c, h):
         at = pl.ds(h * part_rows, part_rows)
@@ -74,8 +90,10 @@
         for h in range(parts):
             for copy in loads(c, h):
                 copy.start()
-    table.start()
-    sizes.wait()
+    read_table.wait()
+    words[...] = table[...] * TROWS
+    give_rows.start()
+    read_sizes.wait()
     for c in range(channels):
         size = size_ref[c]
         for h in range(parts):
@@ -95,70 +113,40 @@
                         ]
 
             loop(part_rows // ROWS, block, unroll=2)
-    table.wait()
+    give_rows.wait()
 
     def store(q):
-        at = pl.ds(q * out_slots, out_slots)
+        at = pl.ds(q * out_places * capacity, out_places * capacity)
         return pltpu.make_async_copy(out.at[at], out_hbm.at[at], out_sem.at[q])
 
+    def pick(slot, row):
+        g = rows[pl.ds(row, TROWS), :]
+        h = rows[pl.ds(row + half, TROWS), :]
+        out[slot] = jnp.concatenate([g, h], axis=0).astype(jnp.bfloat16)
+
     for q in range(out_parts):
-
-        def pick(i, q=q):
-            first_slot = q * out_slots + i * SLOTS
-            for u in range(SLOTS):
-                first = pl.multiple_of(table_ref[0, first_slot + u] * TROWS, TROWS)
-                g = rows[pl.ds(first, TROWS), :]
-                h = rows[pl.ds(first + half, TROWS), :]
-                out[first_slot + u] = jnp.concatenate([g, h], axis=0).astype(jnp.bfloat16)
-
-        loop(out_slots // SLOTS, pick)
+        each_slot(first_rows, q * out_places, out_places, pick)
         store(q).start()
     for q in range(out_parts):
         store(q).wait()
 
 
-def rows_kernel(send_ref, receive_ref, send_rows, receive_rows):
-    pairs = send_rows.shape[1]
-
-    def one(i):
-        for table, packed in ((send_ref, send_rows), (receive_ref, receive_rows)):
-            low = table[0, i] * TROWS
-            packed[0, i] = low + table[0, i + pairs] * (TROWS << HALF_WORD)
-
-    loop(pairs, one, unroll=8)
-
-
-def each_slot(packed, start, count, body):
-    pairs = packed.shape[1]
-
-    def several(i):
-        for u in range(PAIRS_A_TURN):
-            slot = start + i * PAIRS_A_TURN + u
-            word = packed[0, slot]
-            low = pl.multiple_of(word & ((1 << HALF_WORD) - 1), TROWS)
-            high = pl.multiple_of(lax.shift_right_logical(word, HALF_WORD), TROWS)
-            body(slot, low)
-            body(slot + pairs, high)
-
-    loop(count // PAIRS_A_TURN, several)
-
-
-def paired_copies(source, target, sem, q):
-    half = source.shape[0] // 2
-    part = half // sem.shape[1]
-    copies = []
-    for k in range(2):
-        at = pl.ds(k * half + q * part, part)
-        copies.append(pltpu.make_async_copy(source.at[at], target.at[at], sem.at[k, q]))
-    return copies
-
-
-def cross_kernel(packed, weight_ref, in_hbm, out_hbm, arrived, both_rows, gen, ham, wgen, wham, spread_weight, crossed_rows, out, in_sem, out_sem):
+def each_slot(first_rows, start, count, body):
+    capacity = first_rows.shape[1] // DEVICES
+    for place in range(start, start + count):
+        for k in range(capacity):
+            row = first_rows[0, ORDER[place] * capacity + k]
+            body(place * capacity + k, pl.multiple_of(row, TROWS))
+
+
+def cross_kernel(table, weight_ref, arrived, out_hbm, words, first_rows, both_rows, gen, ham, wgen, wham, spread_weight, crossed_rows, out, small_sem, out_sem):
     channels, extent = weight_ref.shape
     panels = extent // LANES
     other = both_rows.shape[0] // 2
-    parts = in_sem.shape[1]
-    part_pairs = packed.shape[1] // parts
+    parts = out_sem.shape[0]
+    part_places = DEVICES // parts
+    part_slots = out.shape[0] // parts
+    give_rows = pltpu.make_async_copy(words, first_rows, small_sem)
 
     def place(slot, row):
         both = arrived[slot].astype(jnp.float32)
@@ -168,15 +156,16 @@
     def give(slot, row):
         out[slot] = crossed_rows[pl.ds(row, TROWS), :].astype(jnp.bfloat16)
 
-    for q in range(parts):
-        for copy in paired_copies(in_hbm, arrived, in_sem, q):
-            copy.start()
+    def store(q):
+        at = pl.ds(q * part_slots, part_slots)
+        return pltpu.make_async_copy(out.at[at], out_hbm.at[at], out_sem.at[q])
+
+    words[...] = table[...] * TROWS
+    give_rows.start()
     for c in range(channels):
         spread(weight_ref[c : c + 1, :], spread_weight.at[c])
-    for q in range(parts):
-        for copy in paired_copies(in_hbm, arrived, in_sem, q):
-            copy.wait()
-        each_slot(packed, q * part_pairs, part_pairs, place)
+    give_rows.wait()
+    each_slot(first_rows, 0, DEVICES, place)
     for c in range(channels):
 
         def block(b, c=c):
@@ -213,12 +202,10 @@
                 ] = product[:, i * LANES : (i + 1) * LANES]
 
     for q in range(parts):
-        each_slot(packed, q * part_pairs, part_pairs, give)
-        for copy in paired_copies(out, out_hbm, out_sem, q):
-            copy.start()
+        each_slot(first_rows, q * part_places, part_places, give)
+        store(q).start()
     for q in range(parts):
-        for copy in paired_copies(out, out_hbm, out_sem, q):
-            copy.wait()
+        store(q).wait()
 
 
 def ladder_kernel(size_ref, weight_ref, gen_ref, ham_ref, out_ref, gen, ham, wgen, wham, spread_weight):
@@ -249,13 +236,13 @@
             )
 
 
-def finish_kernel(size_ref, packed, base_hbm, in_hbm, out_hbm, base, arrived, back_rows, out, base_sem, in_sem, out_sem):
+def finish_kernel(size_hbm, table, base_hbm, arrived, out_hbm, size_ref, words, first_rows, base, back_rows, out, small_sem, base_sem, out_sem):
     channels, extent, _ = base.shape
     panels = extent // LANES
-    parts = in_sem.shape[1]
-    part_pairs = packed.shape[1] // parts
     cuts = out_sem.shape[1]
     cut_rows = extent // cuts
+    give_rows = pltpu.make_async_copy(words, first_rows, small_sem.at[0])
+    read_sizes = pltpu.make_async_copy(size_hbm, size_ref, small_sem.at[1])
 
     def load_base(c):
         return pltpu.make_async_copy(base_hbm.at[c], base.at[c], base_sem.at[c])
@@ -267,15 +254,14 @@
     def place(slot, row):
         back_rows[pl.ds(row, TROWS), :] = arrived[slot].astype(jnp.float32)
 
-    for q in range(parts):
-        for copy in paired_copies(in_hbm, arrived, in_sem, q):
-            copy.start()
+    words[...] = table[...] * TROWS
+    give_rows.start()
+    read_sizes.start()
     for c in range(channels):
         load_base(c).start()
-    for q in range(parts):
-        for copy in paired_copies(in_hbm, arrived, in_sem, q):
-            copy.wait()
-        each_slot(packed, q * part_pairs, part_pairs, place)
+    give_rows.wait()
+    each_slot(first_rows, 0, DEVICES, place)
+    read_sizes.wait()
     for c in range(channels):
         size = size_ref[c]
         load_base(c).wait()
@@ -322,16 +308,18 @@
         out_specs=HBM(),
         scratch_shapes=[
             pltpu.SMEM(channel_size.shape, jnp.int32),
-            pltpu.SMEM(send_table.shape, jnp.int32),
+            pltpu.VMEM(send_table.shape, jnp.int32),
+            pltpu.VMEM((1, slots), jnp.int32),
+            pltpu.SMEM((1, slots), jnp.int32),
             pltpu.VMEM((channels, extent, extent), bf16),
             pltpu.VMEM((channels, extent, extent), bf16),
             pltpu.VMEM((2 * lane_rows, LANES), f32),
             pltpu.VMEM((slots, 2 * TROWS, LANES), bf16),
-            pltpu.SemaphoreType.DMA((2,)),
+            pltpu.SemaphoreType.DMA((3,)),
             pltpu.SemaphoreType.DMA((2, 2 * channels)),
             pltpu.SemaphoreType.DMA((parts,)),
         ],
-        compiler_params=params(60),
+        compiler_params=params(PACK_MIB),
         name="pack",
     )(channel_size, send_table, generator, hamiltonian)
 
@@ -342,19 +330,11 @@
             split_axis=0,
             concat_axis=0,
             tiled=True,
+            axis_index_groups=[ORDER],
         )
         return swapped.reshape(tiles.shape)
 
     arrived = exchange(outgoing)
-
-    send_rows, receive_rows = pl.pallas_call(
-        rows_kernel,
-        out_shape=[jax.ShapeDtypeStruct((1, slots // 2), jnp.int32)] * 2,
-        in_specs=[SMEM(), SMEM()],
-        out_specs=[SMEM(), SMEM()],
-        compiler_params=params(2),
-        name="rows",
-    )(send_table, receive_table)
 
     base = pl.pallas_call(
         ladder_kernel,
@@ -363,50 +343,53 @@
         out_specs=WHOLE(),
         scratch_shapes=[pltpu.VMEM((extent, extent), bf16)] * 4
         + [pltpu.VMEM((extent, LANES), f32)],
-        compiler_params=params(20),
+        compiler_params=params(LADDER_MIB),
         name="ladder",
     )(channel_size, pair_weight, generator, hamiltonian)
 
+    table_words = [
+        pltpu.VMEM((1, slots), jnp.int32),
+        pltpu.SMEM((1, slots), jnp.int32),
+    ]
     going_back = pl.pallas_call(
         cross_kernel,
         out_shape=jax.ShapeDtypeStruct((slots, TROWS, LANES), bf16),
-        in_specs=[SMEM(), WHOLE(), HBM()],
+        in_specs=[WHOLE(), WHOLE(), WHOLE()],
         out_specs=HBM(),
-        scratch_shapes=[
-            pltpu.VMEM((slots, 2 * TROWS, LANES), bf16),
-            pltpu.VMEM((2 * lane_rows, LANES), f32),
-        ]
+        scratch_shapes=table_words
+        + [pltpu.VMEM((2 * lane_rows, LANES), f32)]
         + [pltpu.VMEM((extent, extent), bf16)] * 4
         + [
             pltpu.VMEM((channels, extent, LANES), f32),
             pltpu.VMEM((lane_rows, LANES), f32),
             pltpu.VMEM((slots, TROWS, LANES), bf16),
-            pltpu.SemaphoreType.DMA((2, parts)),
-            pltpu.SemaphoreType.DMA((2, parts)),
+            pltpu.SemaphoreType.DMA,
+            pltpu.SemaphoreType.DMA((parts,)),
         ],
-        compiler_params=params(60),
+        compiler_params=params(CROSS_MIB),
         name="cross",
-    )(receive_rows, cross_weight, arrived)
+    )(receive_table, cross_weight, arrived)
 
     came_back = exchange(going_back)
 
     return pl.pallas_call(
         finish_kernel,
         out_shape=jax.ShapeDtypeStruct((channels, extent, extent), f32),
-        in_specs=[SMEM(), SMEM(), HBM(), HBM()],
+        in_specs=[HBM(), WHOLE(), HBM(), WHOLE()],
         out_specs=HBM(),
-        scratch_shapes=[
+        scratch_shapes=[pltpu.SMEM(channel_size.shape, jnp.int32)]
+        + table_words
+        + [
             pltpu.VMEM((channels, extent, extent), f32),
-            pltpu.VMEM((slots, TROWS, LANES), bf16),
             pltpu.VMEM((lane_rows, LANES), f32),
             pltpu.VMEM((channels, extent, extent), f32),
+            pltpu.SemaphoreType.DMA((2,)),
             pltpu.SemaphoreType.DMA((channels,)),
-            pltpu.SemaphoreType.DMA((2, parts)),
             pltpu.SemaphoreType.DMA((channels, 4)),
         ],
-        compiler_params=params(60),
+        compiler_params=params(FINISH_MIB),
         name="finish",
-    )(channel_size, send_rows, base, came_back)
+    )(channel_size, send_table, base, came_back)
 
 
 def solution(mesh):

time: 171 us -> 159 us (0.930)
  blocking collectives: 0 us -> 91.4 us
  waiting for transfers between devices: 108 us -> 31.3 us
  starting transfers between devices: 21.4 us -> 5.01 us
  Pallas kernels: 35.9 us -> 25.1 us
    all_to_all x0 -> x1, blocking collectives: none -> 91.4 us  [exchange(): lax.all_to_all(tiles.reshape(devices, slots // devices, *tiles.shape[1:])...]
    all_to_all x2 -> x1, waiting for transfers between devices: 108 us -> 31.3 us  [exchange(): lax.all_to_all(tiles.reshape(devices, slots // devices, *tiles.shape[1:])...]
    all_to_all x2 -> x1, starting transfers between devices: 21.4 us -> 5.01 us  [exchange(): lax.all_to_all(tiles.reshape(devices, slots // devices, *tiles.shape[1:])...]
    pallas_call x1 -> x0, Pallas kernels: 5.5 us -> none  [per_device(): pl.pallas_call(rows_kernel, out_shape=[jax.ShapeDtypeStruct((1, slots //...]
    pallas_call x1, Pallas kernels: 11.6 us -> 8.55 us  [per_device(): pl.pallas_call(cross_kernel, out_shape=jax.ShapeDtypeStruct((slots, TROWS...]
    pallas_call x1, Pallas kernels: 6.17 us -> 4.07 us  [per_device(): pl.pallas_call(finish_kernel, out_shape=jax.ShapeDtypeStruct((channels, e...]
    unnamed x18 -> x16, local copies, waits for them, and re-layouts: 4.99 us -> 5.48 us
  transfers between devices with their start and end apart: 2 -> 1, of which waited for: 2 -> 1; matrix products, arithmetic and copies ran while one was open for 0% -> 0% of each run, Pallas kernels for 7% -> 4%
where the time goes in v3:
time: 159 us
  blocking collectives  91.4 us (57%)
  waiting for transfers between devices  31.3 us (20%)
  Pallas kernels  25.1 us (16%)
  local copies, waits for them, and re-layouts  5.48 us (3%)
  starting transfers between devices  5.01 us (3%)
    all_to_all x1, blocking collectives, exchange(): lax.all_to_all(tiles.reshape(devices, slots // devices, *tiles.shape[1:])...  91.4 us
    all_to_all x1, waiting for transfers between devices, exchange(): lax.all_to_all(tiles.reshape(devices, slots // devices, *tiles.shape[1:])...  31.3 us
    pallas_call x1, Pallas kernels, per_device(): pl.pallas_call(cross_kernel, out_shape=jax.ShapeDtypeStruct((slots, TROWS...  8.55 us
    pallas_call x1, Pallas kernels, per_device(): pl.pallas_call(ladder_kernel, out_shape=jax.ShapeDtypeStruct((channels, e...  6.49 us
    pallas_call x1, Pallas kernels, per_device(): pl.pallas_call(pack_kernel, out_shape=jax.ShapeDtypeStruct((slots, 2 * TR...  6 us
    unnamed x16, local copies, waits for them, and re-layouts  5.48 us
    all_to_all x1, starting transfers between devices, exchange(): lax.all_to_all(tiles.reshape(devices, slots // devices, *tiles.shape[1:])...  5.01 us
    pallas_call x1, Pallas kernels, per_device(): pl.pallas_call(finish_kernel, out_shape=jax.ShapeDtypeStruct((channels, e...  4.07 us
  transfers between devices with their start and end apart: 1, of which 1 were waited for; matrix products, arithmetic and copies ran while one was open for 0% of the time, Pallas kernels for 4%

profile of v3, /device:TPU:1, one launch (start us, length us, event | category | flops | bytes accessed | tf_op | source)
XLA Modules:
  0.0 158.6 jit_solution(15235275768790959254)
XLA Ops:
  0.0 6.0 %pack.1 = bf16[1664,16,128]{2,1,0:T(8,128)(2,1)} custom-call(s32[2]{0:T(128)} %size_hbm.3, s32[1,1664]{1,0:T(1,128)} %table.3, bf16[2,768,768]{2,1,0:T(8,128)(2,1)} %gen_hbm.1, bf16[2,768,768]{2,1,0:T(8,128)(2,1)} %ham_hbm.1), custom_call_target="tpu_custom_call" | custom-call | tf_op jit(solution)/shard_map/pack/pallas_call | solution.py:304
  6.0 0.0 copy-start.4
  6.0 0.0 copy-start.5
  6.0 91.4 %all_to_all.10 = bf16[128,13,16,128]{3,2,1,0:T(8,128)(2,1)S(1)} all-to-all(bf16[128,13,16,128]{3,2,1,0:T(8,128)(2,1)} %bitcast.6), channel_id=1, replica_groups={{0,32,64,96,2,34,66,98,4,36,68,100,6,38,70,102,1,33,65,97,3,35,67,99,5,..., dimensions={0} | all-to-all | bytes 13631488 | tf_op jit(solution)/shard_map/all_to_all | solution.py:327
  97.4 0.0 copy-done.4
  97.4 0.0 copy-done.5
  97.4 8.5 %cross.1 = bf16[1664,8,128]{2,1,0:T(8,128)(2,1)} custom-call(s32[1,1664]{1,0:T(1,128)S(1)} %copy-done.4, f32[2,768]{1,0:T(2,128)S(1)} %copy-done.5, bf16[1664,16,128]{2,1,0:T(8,128)(2,1)S(1)} %bitcast.4), custom_call_target="tpu_custom_call" | custom-call | tf_op jit(solution)/shard_map/cross/pallas_call | solution.py:354
  106.0 0.0 copy-start.6
  106.0 0.0 copy-start.7
  106.0 5.0 %all-to-all-start.1 = ((bf16[128,13,8,128]{3,2,1,0:T(8,128)(2,1)}), bf16[128,13,8,128]{3,2,1,0:T(8,128)(2,1)S(1)}, u32[]{:S(2)}, u32[]{:S(2)}) async-start(bf16[128,13,8,128]{3,2,1,0:T(8,128)(2,1)} %bitcast.2), calls=%async_computation.1 | async-start | bytes 6815744 | tf_op jit(solution)/shard_map/all_to_all | solution.py:327
  111.0 0.0 copy-done.6
  111.0 0.0 copy-done.7
  111.0 0.0 copy-start.1
  111.0 1.7 %copy-done.1 = bf16[2,768,768]{2,1,0:T(8,128)(2,1)S(1)} copy-done((bf16[2,768,768]{2,1,0:T(8,128)(2,1)S(1)}, bf16[2,768,768]{2,1,0:T(8,128)(2,1)}, u32[]{:S(2)}) %copy-start.1) | copy-done | bytes 2359320
  112.7 0.0 copy-start.2
  112.7 1.7 %copy-done.2 = bf16[2,768,768]{2,1,0:T(8,128)(2,1)S(1)} copy-done((bf16[2,768,768]{2,1,0:T(8,128)(2,1)S(1)}, bf16[2,768,768]{2,1,0:T(8,128)(2,1)}, u32[]{:S(2)}) %copy-start.2) | copy-done | bytes 2359320
  114.4 0.0 copy-start.3
  114.4 6.5 %ladder.1.base_hbm = f32[2,768,768]{2,1,0:T(8,128)S(1)} custom-call(s32[2]{0:T(128)S(1)} %copy-done.7, f32[2,768]{1,0:T(2,128)S(1)} %copy-done.6, bf16[2,768,768]{2,1,0:T(8,128)(2,1)S(1)} %copy-done.1, bf16[2,768,768]{2,1,0:T(8,128)(2,1)S(1)} %copy-done.2), custom_call_target="tpu_custom_call" | custom-call | tf_op jit(solution)/shard_map/ladder/pallas_call | solution.py:339
  120.9 0.0 copy-start
  120.9 2.1 %copy-done = f32[2,768,768]{2,1,0:T(8,128)} copy-done((f32[2,768,768]{2,1,0:T(8,128)}, f32[2,768,768]{2,1,0:T(8,128)S(1)}, u32[]{:S(2)}) %copy-start) | copy-done | bytes 4718616
  123.0 31.3 %all-to-all-done.1 = bf16[128,13,8,128]{3,2,1,0:T(8,128)(2,1)S(1)} async-done(((bf16[128,13,8,128]{3,2,1,0:T(8,128)(2,1)}), bf16[128,13,8,128]{3,2,1,0:T(8,128)(2,1)S(1)}, u32[]{:S(2)}, u32[]{:S(2)}) %all-to-all-start.1) | async-done | bytes 3407904 | tf_op jit(solution)/shard_map/all_to_all | solution.py:327
  154.3 0.0 copy-done.3
  154.3 4.1 %finish.1 = f32[2,768,768]{2,1,0:T(8,128)} custom-call(s32[2]{0:T(128)S(1)} %copy-done.7, s32[1,1664]{1,0:T(1,128)S(1)} %copy-done.3, f32[2,768,768]{2,1,0:T(8,128)} %copy-done, bf16[1664,8,128]{2,1,0:T(8,128)(2,1)S(1)} %bitcast.5), custom_call_target="tpu_custom_call" | custom-call | tf_op jit(solution)/shard_map/finish/pallas_call | solution.py:375
Async XLA Ops:
  6.0 91.4 %copy-start.4 = (s32[1,1664]{1,0:T(1,128)S(1)}, s32[1,1664]{1,0:T(1,128)}, u32[]{:S(2)}) copy-start(s32[1,1664]{1,0:T(1,128)} %table.2) | copy-start | bytes 19972
  6.0 91.4 %copy-start.5 = (f32[2,768]{1,0:T(2,128)S(1)}, f32[2,768]{1,0:T(2,128)}, u32[]{:S(2)}) copy-start(f32[2,768]{1,0:T(2,128)} %weight_ref.3) | copy-start | bytes 18436
  106.0 5.0 %copy-start.6 = (f32[2,768]{1,0:T(2,128)S(1)}, f32[2,768]{1,0:T(2,128)}, u32[]{:S(2)}) copy-start(f32[2,768]{1,0:T(2,128)} %weight_ref.2) | copy-start | bytes 18436
  106.0 5.0 %copy-start.7 = (s32[2]{0:T(128)S(1)}, s32[2]{0:T(128)}, u32[]{:S(2)}) copy-start(s32[2]{0:T(128)} %size_hbm.3) | copy-start | bytes 28
  106.0 48.3 %all-to-all-start.1 = ((bf16[128,13,8,128]{3,2,1,0:T(8,128)(2,1)}), bf16[128,13,8,128]{3,2,1,0:T(8,128)(2,1)S(1)}, u32[]{:S(2)}, u32[]{:S(2)}) async-start(bf16[128,13,8,128]{3,2,1,0:T(8,128)(2,1)} %bitcast.2), calls=%async_computation.1 | async-start | bytes 6815744 | tf_op jit(solution)/shard_map/all_to_all | solution.py:327
  111.0 1.7 %copy-start.1 = (bf16[2,768,768]{2,1,0:T(8,128)(2,1)S(1)}, bf16[2,768,768]{2,1,0:T(8,128)(2,1)}, u32[]{:S(2)}) copy-start(bf16[2,768,768]{2,1,0:T(8,128)(2,1)} %gen_hbm.1) | copy-start | bytes 7077892
  112.7 1.7 %copy-start.2 = (bf16[2,768,768]{2,1,0:T(8,128)(2,1)S(1)}, bf16[2,768,768]{2,1,0:T(8,128)(2,1)}, u32[]{:S(2)}) copy-start(bf16[2,768,768]{2,1,0:T(8,128)(2,1)} %ham_hbm.1) | copy-start | bytes 7077892
  114.4 40.0 %copy-start.3 = (s32[1,1664]{1,0:T(1,128)S(1)}, s32[1,1664]{1,0:T(1,128)}, u32[]{:S(2)}) copy-start(s32[1,1664]{1,0:T(1,128)} %table.3) | copy-start | bytes 19972
  120.9 2.1 %copy-start = (f32[2,768,768]{2,1,0:T(8,128)}, f32[2,768,768]{2,1,0:T(8,128)S(1)}, u32[]{:S(2)}) copy-start(f32[2,768,768]{2,1,0:T(8,128)S(1)} %ladder.1.base_hbm) | copy-start | bytes 14155780

commit v4 on v3

--- a/solution.py
+++ b/solution.py
@@ -14,7 +14,7 @@
 
 flow_step = 0.5
 
-PACK_MIB, LADDER_MIB, CROSS_MIB, FINISH_MIB = 60, 20, 40, 50
+PACK_MIB, LADDER_MIB, CROSS_MIB, FINISH_MIB = 40, 20, 40, 50
 
 AXES = ("group", "chan")
 X_BITS, Y_BITS, Z_BITS, CORE_BITS = 2, 2, 2, 1
@@ -63,15 +63,11 @@
         )
 
 
-def pack_kernel(size_hbm, table_hbm, gen_hbm, ham_hbm, out_hbm, size_ref, table, words, first_rows, gen, ham, rows, out, small_sem, in_sem, out_sem):
+def pack_kernel(size_hbm, table_hbm, gen_hbm, ham_hbm, out, size_ref, table, words, first_rows, gen, ham, rows, small_sem, in_sem):
     channels, extent, _ = gen.shape
     panels = extent // LANES
     half = rows.shape[0] // 2
     parts, part_rows = chunks_of(extent, 2)
-    capacity = first_rows.shape[1] // DEVICES
-    out_parts = out_sem.shape[0]
-    out_places = DEVICES // out_parts
-
     read_table = pltpu.make_async_copy(table_hbm, table, small_sem.at[0])
     read_sizes = pltpu.make_async_copy(size_hbm, size_ref, small_sem.at[1])
     give_rows = pltpu.make_async_copy(words, first_rows, small_sem.at[2])
@@ -115,20 +111,12 @@
             loop(part_rows // ROWS, block, unroll=2)
     give_rows.wait()
 
-    def store(q):
-        at = pl.ds(q * out_places * capacity, out_places * capacity)
-        return pltpu.make_async_copy(out.at[at], out_hbm.at[at], out_sem.at[q])
-
     def pick(slot, row):
         g = rows[pl.ds(row, TROWS), :]
         h = rows[pl.ds(row + half, TROWS), :]
         out[slot] = jnp.concatenate([g, h], axis=0).astype(jnp.bfloat16)
 
-    for q in range(out_parts):
-        each_slot(first_rows, q * out_places, out_places, pick)
-        store(q).start()
-    for q in range(out_parts):
-        store(q).wait()
+    each_slot(first_rows, 0, DEVICES, pick)
 
 
 def each_slot(first_rows, start, count, body):
@@ -290,6 +278,10 @@
 WHOLE = functools.partial(pl.BlockSpec, memory_space=pltpu.VMEM)
 
 
+def in_hbm(operand):
+    return pltpu.with_memory_space_constraint(operand, pltpu.HBM)
+
+
 def per_device(
     generator, hamiltonian, pair_weight, cross_weight, channel_size, send_table, receive_table
 ):
@@ -305,7 +297,7 @@
         pack_kernel,
         out_shape=jax.ShapeDtypeStruct((slots, 2 * TROWS, LANES), bf16),
         in_specs=[HBM()] * 4,
-        out_specs=HBM(),
+        out_specs=WHOLE(),
         scratch_shapes=[
             pltpu.SMEM(channel_size.shape, jnp.int32),
             pltpu.VMEM(send_table.shape, jnp.int32),
@@ -314,14 +306,12 @@
             pltpu.VMEM((channels, extent, extent), bf16),
             pltpu.VMEM((channels, extent, extent), bf16),
             pltpu.VMEM((2 * lane_rows, LANES), f32),
-            pltpu.VMEM((slots, 2 * TROWS, LANES), bf16),
             pltpu.SemaphoreType.DMA((3,)),
             pltpu.SemaphoreType.DMA((2, 2 * channels)),
-            pltpu.SemaphoreType.DMA((parts,)),
         ],
         compiler_params=params(PACK_MIB),
         name="pack",
-    )(channel_size, send_table, generator, hamiltonian)
+    )(*(in_hbm(v) for v in (channel_size, send_table, generator, hamiltonian)))
 
     def exchange(tiles):
         swapped = lax.all_to_all(
@@ -389,7 +379,7 @@
         ],
         compiler_params=params(FINISH_MIB),
         name="finish",
-    )(channel_size, send_table, base, came_back)
+    )(channel_size, send_table, in_hbm(base), came_back)
 
 
 def solution(mesh):

time: 159 us -> 156 us (0.981)
  Pallas kernels: 25.1 us -> 23 us
    pallas_call x1, Pallas kernels: 6 us -> 3.91 us  [per_device(): pl.pallas_call(pack_kernel, out_shape=jax.ShapeDtypeStruct((slots, 2 * TR...]
where the time goes in v4:
time: 156 us
  blocking collectives  91.2 us (58%)
  waiting for transfers between devices  31.3 us (20%)
  Pallas kernels  23 us (15%)
  local copies, waits for them, and re-layouts  5.48 us (4%)
  starting transfers between devices  5.01 us (3%)
    all_to_all x1, blocking collectives, exchange(): lax.all_to_all(tiles.reshape(devices, slots // devices, *tiles.shape[1:])...  91.2 us
    all_to_all x1, waiting for transfers between devices, exchange(): lax.all_to_all(tiles.reshape(devices, slots // devices, *tiles.shape[1:])...  31.3 us
    pallas_call x1, Pallas kernels, per_device(): pl.pallas_call(cross_kernel, out_shape=jax.ShapeDtypeStruct((slots, TROWS...  8.55 us
    pallas_call x1, Pallas kernels, per_device(): pl.pallas_call(ladder_kernel, out_shape=jax.ShapeDtypeStruct((channels, e...  6.49 us
    unnamed x16, local copies, waits for them, and re-layouts  5.48 us
    all_to_all x1, starting transfers between devices, exchange(): lax.all_to_all(tiles.reshape(devices, slots // devices, *tiles.shape[1:])...  5.01 us
    pallas_call x1, Pallas kernels, per_device(): pl.pallas_call(finish_kernel, out_shape=jax.ShapeDtypeStruct((channels, e...  4.07 us
    pallas_call x1, Pallas kernels, per_device(): pl.pallas_call(pack_kernel, out_shape=jax.ShapeDtypeStruct((slots, 2 * TR...  3.91 us
  transfers between devices with their start and end apart: 1, of which 1 were waited for; matrix products, arithmetic and copies ran while one was open for 0% of the time, Pallas kernels for 4%

profile of v4, /device:TPU:1, one launch (start us, length us, event | category | flops | bytes accessed | tf_op | source)
XLA Modules:
  0.0 156.1 jit_solution(10190638818536270516)
XLA Ops:
  0.0 3.9 %pack.1 = bf16[1664,16,128]{2,1,0:T(8,128)(2,1)S(1)} custom-call(s32[2]{0:T(128)} %size_hbm.3, s32[1,1664]{1,0:T(1,128)} %table.3, bf16[2,768,768]{2,1,0:T(8,128)(2,1)} %gen_hbm.1, bf16[2,768,768]{2,1,0:T(8,128)(2,1)} %ham_hbm.1), custom_call_target="tpu_custom_call" | custom-call | tf_op jit(solution)/shard_map/pack/pallas_call | solution.py:296
  3.9 0.0 copy-start.4
  3.9 0.0 copy-start.5
  3.9 91.2 %all_to_all.10 = bf16[128,13,16,128]{3,2,1,0:T(8,128)(2,1)S(1)} all-to-all(bf16[128,13,16,128]{3,2,1,0:T(8,128)(2,1)S(1)} %bitcast.4), channel_id=1, replica_groups={{0,32,64,96,2,34,66,98,4,36,68,100,6,38,70,102,1,33,65,97,3,35,67,99,5,..., dimensions={0} | all-to-all | bytes 13631488 | tf_op jit(solution)/shard_map/all_to_all | solution.py:317
  95.1 0.0 copy-done.4
  95.1 0.0 copy-done.5
  95.1 8.5 %cross.1 = bf16[1664,8,128]{2,1,0:T(8,128)(2,1)} custom-call(s32[1,1664]{1,0:T(1,128)S(1)} %copy-done.4, f32[2,768]{1,0:T(2,128)S(1)} %copy-done.5, bf16[1664,16,128]{2,1,0:T(8,128)(2,1)S(1)} %bitcast.5), custom_call_target="tpu_custom_call" | custom-call | tf_op jit(solution)/shard_map/cross/pallas_call | solution.py:344
  103.6 0.0 copy-start.6
  103.7 0.0 copy-start.7
  103.7 5.0 %all-to-all-start.1 = ((bf16[128,13,8,128]{3,2,1,0:T(8,128)(2,1)}), bf16[128,13,8,128]{3,2,1,0:T(8,128)(2,1)S(1)}, u32[]{:S(2)}, u32[]{:S(2)}) async-start(bf16[128,13,8,128]{3,2,1,0:T(8,128)(2,1)} %bitcast.2), calls=%async_computation.1 | async-start | bytes 6815744 | tf_op jit(solution)/shard_map/all_to_all | solution.py:317
  108.7 0.0 copy-done.6
  108.7 0.0 copy-done.7
  108.7 0.0 copy-start.1
  108.7 1.7 %copy-done.1 = bf16[2,768,768]{2,1,0:T(8,128)(2,1)S(1)} copy-done((bf16[2,768,768]{2,1,0:T(8,128)(2,1)S(1)}, bf16[2,768,768]{2,1,0:T(8,128)(2,1)}, u32[]{:S(2)}) %copy-start.1) | copy-done | bytes 2359320
  110.4 0.0 copy-start.2
  110.4 1.7 %copy-done.2 = bf16[2,768,768]{2,1,0:T(8,128)(2,1)S(1)} copy-done((bf16[2,768,768]{2,1,0:T(8,128)(2,1)S(1)}, bf16[2,768,768]{2,1,0:T(8,128)(2,1)}, u32[]{:S(2)}) %copy-start.2) | copy-done | bytes 2359320
  112.0 0.0 copy-start.3
  112.0 6.5 %ladder.1.base_hbm = f32[2,768,768]{2,1,0:T(8,128)S(1)} custom-call(s32[2]{0:T(128)S(1)} %copy-done.7, f32[2,768]{1,0:T(2,128)S(1)} %copy-done.6, bf16[2,768,768]{2,1,0:T(8,128)(2,1)S(1)} %copy-done.1, bf16[2,768,768]{2,1,0:T(8,128)(2,1)S(1)} %copy-done.2), custom_call_target="tpu_custom_call" | custom-call | tf_op jit(solution)/shard_map/ladder/pallas_call | solution.py:329
  118.5 0.0 copy-start
  118.6 2.1 %copy-done = f32[2,768,768]{2,1,0:T(8,128)} copy-done((f32[2,768,768]{2,1,0:T(8,128)}, f32[2,768,768]{2,1,0:T(8,128)S(1)}, u32[]{:S(2)}) %copy-start) | copy-done | bytes 4718616
  120.7 31.3 %all-to-all-done.1 = bf16[128,13,8,128]{3,2,1,0:T(8,128)(2,1)S(1)} async-done(((bf16[128,13,8,128]{3,2,1,0:T(8,128)(2,1)}), bf16[128,13,8,128]{3,2,1,0:T(8,128)(2,1)S(1)}, u32[]{:S(2)}, u32[]{:S(2)}) %all-to-all-start.1) | async-done | bytes 3407904 | tf_op jit(solution)/shard_map/all_to_all | solution.py:317
  152.0 0.0 copy-done.3
  152.0 4.1 %finish.1 = f32[2,768,768]{2,1,0:T(8,128)} custom-call(s32[2]{0:T(128)S(1)} %copy-done.7, s32[1,1664]{1,0:T(1,128)S(1)} %copy-done.3, f32[2,768,768]{2,1,0:T(8,128)} %copy-done, bf16[1664,8,128]{2,1,0:T(8,128)(2,1)S(1)} %bitcast.6), custom_call_target="tpu_custom_call" | custom-call | tf_op jit(solution)/shard_map/finish/pallas_call | solution.py:365
Async XLA Ops:
  3.9 91.2 %copy-start.4 = (s32[1,1664]{1,0:T(1,128)S(1)}, s32[1,1664]{1,0:T(1,128)}, u32[]{:S(2)}) copy-start(s32[1,1664]{1,0:T(1,128)} %table.2) | copy-start | bytes 19972
  3.9 91.2 %copy-start.5 = (f32[2,768]{1,0:T(2,128)S(1)}, f32[2,768]{1,0:T(2,128)}, u32[]{:S(2)}) copy-start(f32[2,768]{1,0:T(2,128)} %weight_ref.3) | copy-start | bytes 18436
  103.6 5.0 %copy-start.6 = (f32[2,768]{1,0:T(2,128)S(1)}, f32[2,768]{1,0:T(2,128)}, u32[]{:S(2)}) copy-start(f32[2,768]{1,0:T(2,128)} %weight_ref.2) | copy-start | bytes 18436
  103.7 5.0 %copy-start.7 = (s32[2]{0:T(128)S(1)}, s32[2]{0:T(128)}, u32[]{:S(2)}) copy-start(s32[2]{0:T(128)} %size_hbm.3) | copy-start | bytes 28
  103.7 48.3 %all-to-all-start.1 = ((bf16[128,13,8,128]{3,2,1,0:T(8,128)(2,1)}), bf16[128,13,8,128]{3,2,1,0:T(8,128)(2,1)S(1)}, u32[]{:S(2)}, u32[]{:S(2)}) async-start(bf16[128,13,8,128]{3,2,1,0:T(8,128)(2,1)} %bitcast.2), calls=%async_computation.1 | async-start | bytes 6815744 | tf_op jit(solution)/shard_map/all_to_all | solution.py:317
  108.7 1.7 %copy-start.1 = (bf16[2,768,768]{2,1,0:T(8,128)(2,1)S(1)}, bf16[2,768,768]{2,1,0:T(8,128)(2,1)}, u32[]{:S(2)}) copy-start(bf16[2,768,768]{2,1,0:T(8,128)(2,1)} %gen_hbm.1) | copy-start | bytes 7077892
  110.4 1.7 %copy-start.2 = (bf16[2,768,768]{2,1,0:T(8,128)(2,1)S(1)}, bf16[2,768,768]{2,1,0:T(8,128)(2,1)}, u32[]{:S(2)}) copy-start(bf16[2,768,768]{2,1,0:T(8,128)(2,1)} %ham_hbm.1) | copy-start | bytes 7077892
  112.0 40.0 %copy-start.3 = (s32[1,1664]{1,0:T(1,128)S(1)}, s32[1,1664]{1,0:T(1,128)}, u32[]{:S(2)}) copy-start(s32[1,1664]{1,0:T(1,128)} %table.3) | copy-start | bytes 19972
  118.5 2.1 %copy-start = (f32[2,768,768]{2,1,0:T(8,128)}, f32[2,768,768]{2,1,0:T(8,128)S(1)}, u32[]{:S(2)}) copy-start(f32[2,768,768]{2,1,0:T(8,128)S(1)} %ladder.1.base_hbm) | copy-start | bytes 14155780

commit v5 on v4

--- a/solution.py
+++ b/solution.py
@@ -67,7 +67,8 @@
     channels, extent, _ = gen.shape
     panels = extent // LANES
     half = rows.shape[0] // 2
-    parts, part_rows = chunks_of(extent, 2)
+    parts = in_sem.shape[1] // channels
+    part_rows = extent // parts
     read_table = pltpu.make_async_copy(table_hbm, table, small_sem.at[0])
     read_sizes = pltpu.make_async_copy(size_hbm, size_ref, small_sem.at[1])
     give_rows = pltpu.make_async_copy(words, first_rows, small_sem.at[2])
@@ -154,40 +155,45 @@
         spread(weight_ref[c : c + 1, :], spread_weight.at[c])
     give_rows.wait()
     each_slot(first_rows, 0, DEVICES, place)
-    for c in range(channels):
-
-        def block(b, c=c):
-            first = pl.multiple_of(b * ROWS, ROWS)
-            rows = pl.ds(first, ROWS)
-            base = (c * extent + first) * panels
-            weight = spread_weight[c, rows, :]
-            for p in range(0, panels, 2):
-                lanes = slice(p * LANES, (p + 2) * LANES)
-                g = [both_rows[pl.ds(base + (p + i), ROWS, stride=panels), :] for i in range(2)]
-                h = [
-                    both_rows[pl.ds(base + (other + p + i), ROWS, stride=panels), :]
-                    for i in range(2)
-                ]
-                for target, pair in (
-                    (gen, g),
-                    (ham, h),
-                    (wgen, [weight * x for x in g]),
-                    (wham, [weight * x for x in h]),
-                ):
-                    target[rows, lanes] = jnp.concatenate(pair, axis=1).astype(jnp.bfloat16)
-
-        loop(extent // ROWS, block, unroll=2)
-        step = 2 * LANES
+
+    def relayout(c, first):
+        rows = pl.ds(first, ROWS)
+        base = (c * extent + first) * panels
+        weight = spread_weight[c, rows, :]
+        for p in range(0, panels, 2):
+            lanes = slice(p * LANES, (p + 2) * LANES)
+            g = [both_rows[pl.ds(base + (p + i), ROWS, stride=panels), :] for i in range(2)]
+            h = [
+                both_rows[pl.ds(base + (other + p + i), ROWS, stride=panels), :]
+                for i in range(2)
+            ]
+            for target, pair in (
+                (gen, g),
+                (ham, h),
+                (wgen, [weight * x for x in g]),
+                (wham, [weight * x for x in h]),
+            ):
+                target[c, rows, lanes] = jnp.concatenate(pair, axis=1).astype(jnp.bfloat16)
+
+    def block(b):
+        relayout(0, pl.multiple_of(b * ROWS, ROWS))
+
+    loop(extent // ROWS, block, unroll=2)
+    step = 2 * LANES
+    for c in range(channels):
         for n in range(extent // step):
             columns = slice(n * step, (n + 1) * step)
-            first = jnp.dot(gen[...], wham[:, columns], preferred_element_type=jnp.float32)
-            second = jnp.dot(ham[...], wgen[:, columns], preferred_element_type=jnp.float32)
+            first = jnp.dot(gen[c], wham[c, :, columns], preferred_element_type=jnp.float32)
+            second = jnp.dot(ham[c], wgen[c, :, columns], preferred_element_type=jnp.float32)
             product = first - second
             for i in range(step // LANES):
                 p = n * (step // LANES) + i
                 crossed_rows[
                     pl.ds(c * extent * panels + p, extent, stride=panels), :
                 ] = product[:, i * LANES : (i + 1) * LANES]
+            if c + 1 < channels:
+                for row in range(n * step, (n + 1) * step, ROWS):
+                    relayout(c + 1, row)
 
     for q in range(parts):
         each_slot(first_rows, q * part_places, part_places, give)
@@ -289,7 +295,7 @@
     slots = send_table.shape[1]
     panels = extent // LANES
     lane_rows = channels * extent * panels + TROWS
-    parts = 8
+    parts = 16
     devices = lax.axis_size(AXES)
     f32, bf16 = jnp.float32, jnp.bfloat16
 
@@ -307,7 +313,7 @@
             pltpu.VMEM((channels, extent, extent), bf16),
             pltpu.VMEM((2 * lane_rows, LANES), f32),
             pltpu.SemaphoreType.DMA((3,)),
-            pltpu.SemaphoreType.DMA((2, 2 * channels)),
+            pltpu.SemaphoreType.DMA((2, 4 * channels)),
         ],
         compiler_params=params(PACK_MIB),
         name="pack",
@@ -348,7 +354,7 @@
         out_specs=HBM(),
         scratch_shapes=table_words
         + [pltpu.VMEM((2 * lane_rows, LANES), f32)]
-        + [pltpu.VMEM((extent, extent), bf16)] * 4
+        + [pltpu.VMEM((channels, extent, extent), bf16)] * 4
         + [
             pltpu.VMEM((channels, extent, LANES), f32),
             pltpu.VMEM((lane_rows, LANES), f32),

time: 156 us -> 156 us (level)
  no operation moved by 1% of the time
where the time goes in v5:
time: 156 us
  blocking collectives  91.2 us (58%)
  waiting for transfers between devices  31.3 us (20%)
  Pallas kernels  22.7 us (15%)
  local copies, waits for them, and re-layouts  5.48 us (4%)
  starting transfers between devices  5.01 us (3%)
    all_to_all x1, blocking collectives, exchange(): lax.all_to_all(tiles.reshape(devices, slots // devices, *tiles.shape[1:])...  91.2 us
    all_to_all x1, waiting for transfers between devices, exchange(): lax.all_to_all(tiles.reshape(devices, slots // devices, *tiles.shape[1:])...  31.3 us
    pallas_call x1, Pallas kernels, per_device(): pl.pallas_call(cross_kernel, out_shape=jax.ShapeDtypeStruct((slots, TROWS...  7.96 us
    pallas_call x1, Pallas kernels, per_device(): pl.pallas_call(ladder_kernel, out_shape=jax.ShapeDtypeStruct((channels, e...  6.49 us
    unnamed x16, local copies, waits for them, and re-layouts  5.48 us
    all_to_all x1, starting transfers between devices, exchange(): lax.all_to_all(tiles.reshape(devices, slots // devices, *tiles.shape[1:])...  5.01 us
    pallas_call x1, Pallas kernels, per_device(): pl.pallas_call(pack_kernel, out_shape=jax.ShapeDtypeStruct((slots, 2 * TR...  4.16 us
    pallas_call x1, Pallas kernels, per_device(): pl.pallas_call(finish_kernel, out_shape=jax.ShapeDtypeStruct((channels, e...  4.07 us
  transfers between devices with their start and end apart: 1, of which 1 were waited for; matrix products, arithmetic and copies ran while one was open for 0% of the time, Pallas kernels for 4%

profile of v5, /device:TPU:1, one launch (start us, length us, event | category | flops | bytes accessed | tf_op | source)
XLA Modules:
  0.0 155.9 jit_solution(6113187890636362360)
XLA Ops:
  0.0 4.2 %pack.1 = bf16[1664,16,128]{2,1,0:T(8,128)(2,1)S(1)} custom-call(s32[2]{0:T(128)} %size_hbm.3, s32[1,1664]{1,0:T(1,128)} %table.3, bf16[2,768,768]{2,1,0:T(8,128)(2,1)} %gen_hbm.1, bf16[2,768,768]{2,1,0:T(8,128)(2,1)} %ham_hbm.1), custom_call_target="tpu_custom_call" | custom-call | tf_op jit(solution)/shard_map/pack/pallas_call | solution.py:302
  4.2 0.0 copy-start.4
  4.2 0.0 copy-start.5
  4.2 91.2 %all_to_all.10 = bf16[128,13,16,128]{3,2,1,0:T(8,128)(2,1)S(1)} all-to-all(bf16[128,13,16,128]{3,2,1,0:T(8,128)(2,1)S(1)} %bitcast.4), channel_id=1, replica_groups={{0,32,64,96,2,34,66,98,4,36,68,100,6,38,70,102,1,33,65,97,3,35,67,99,5,..., dimensions={0} | all-to-all | bytes 13631488 | tf_op jit(solution)/shard_map/all_to_all | solution.py:323
  95.3 0.0 copy-done.4
  95.3 0.0 copy-done.5
  95.3 8.0 %cross.1 = bf16[1664,8,128]{2,1,0:T(8,128)(2,1)} custom-call(s32[1,1664]{1,0:T(1,128)S(1)} %copy-done.4, f32[2,768]{1,0:T(2,128)S(1)} %copy-done.5, bf16[1664,16,128]{2,1,0:T(8,128)(2,1)S(1)} %bitcast.5), custom_call_target="tpu_custom_call" | custom-call | tf_op jit(solution)/shard_map/cross/pallas_call | solution.py:350
  103.3 0.0 copy-start.6
  103.3 0.0 copy-start.7
  103.3 5.0 %all-to-all-start.1 = ((bf16[128,13,8,128]{3,2,1,0:T(8,128)(2,1)}), bf16[128,13,8,128]{3,2,1,0:T(8,128)(2,1)S(1)}, u32[]{:S(2)}, u32[]{:S(2)}) async-start(bf16[128,13,8,128]{3,2,1,0:T(8,128)(2,1)} %bitcast.2), calls=%async_computation.1 | async-start | bytes 6815744 | tf_op jit(solution)/shard_map/all_to_all | solution.py:323
  108.4 0.0 copy-done.6
  108.4 0.0 copy-done.7
  108.4 0.0 copy-start.1
  108.4 1.7 %copy-done.1 = bf16[2,768,768]{2,1,0:T(8,128)(2,1)S(1)} copy-done((bf16[2,768,768]{2,1,0:T(8,128)(2,1)S(1)}, bf16[2,768,768]{2,1,0:T(8,128)(2,1)}, u32[]{:S(2)}) %copy-start.1) | copy-done | bytes 2359320
  110.0 0.0 copy-start.2
  110.0 1.7 %copy-done.2 = bf16[2,768,768]{2,1,0:T(8,128)(2,1)S(1)} copy-done((bf16[2,768,768]{2,1,0:T(8,128)(2,1)S(1)}, bf16[2,768,768]{2,1,0:T(8,128)(2,1)}, u32[]{:S(2)}) %copy-start.2) | copy-done | bytes 2359320
  111.7 0.0 copy-start.3
  111.7 6.5 %ladder.1.base_hbm = f32[2,768,768]{2,1,0:T(8,128)S(1)} custom-call(s32[2]{0:T(128)S(1)} %copy-done.7, f32[2,768]{1,0:T(2,128)S(1)} %copy-done.6, bf16[2,768,768]{2,1,0:T(8,128)(2,1)S(1)} %copy-done.1, bf16[2,768,768]{2,1,0:T(8,128)(2,1)S(1)} %copy-done.2), custom_call_target="tpu_custom_call" | custom-call | tf_op jit(solution)/shard_map/ladder/pallas_call | solution.py:335
  118.2 0.0 copy-start
  118.2 2.1 %copy-done = f32[2,768,768]{2,1,0:T(8,128)} copy-done((f32[2,768,768]{2,1,0:T(8,128)}, f32[2,768,768]{2,1,0:T(8,128)S(1)}, u32[]{:S(2)}) %copy-start) | copy-done | bytes 4718616
  120.3 31.3 %all-to-all-done.1 = bf16[128,13,8,128]{3,2,1,0:T(8,128)(2,1)S(1)} async-done(((bf16[128,13,8,128]{3,2,1,0:T(8,128)(2,1)}), bf16[128,13,8,128]{3,2,1,0:T(8,128)(2,1)S(1)}, u32[]{:S(2)}, u32[]{:S(2)}) %all-to-all-start.1) | async-done | bytes 3407904 | tf_op jit(solution)/shard_map/all_to_all | solution.py:323
  151.7 0.0 copy-done.3
  151.7 4.1 %finish.1 = f32[2,768,768]{2,1,0:T(8,128)} custom-call(s32[2]{0:T(128)S(1)} %copy-done.7, s32[1,1664]{1,0:T(1,128)S(1)} %copy-done.3, f32[2,768,768]{2,1,0:T(8,128)} %copy-done, bf16[1664,8,128]{2,1,0:T(8,128)(2,1)S(1)} %bitcast.6), custom_call_target="tpu_custom_call" | custom-call | tf_op jit(solution)/shard_map/finish/pallas_call | solution.py:371
Async XLA Ops:
  4.2 91.2 %copy-start.4 = (s32[1,1664]{1,0:T(1,128)S(1)}, s32[1,1664]{1,0:T(1,128)}, u32[]{:S(2)}) copy-start(s32[1,1664]{1,0:T(1,128)} %table.2) | copy-start | bytes 19972
  4.2 91.2 %copy-start.5 = (f32[2,768]{1,0:T(2,128)S(1)}, f32[2,768]{1,0:T(2,128)}, u32[]{:S(2)}) copy-start(f32[2,768]{1,0:T(2,128)} %weight_ref.3) | copy-start | bytes 18436
  103.3 5.0 %copy-start.6 = (f32[2,768]{1,0:T(2,128)S(1)}, f32[2,768]{1,0:T(2,128)}, u32[]{:S(2)}) copy-start(f32[2,768]{1,0:T(2,128)} %weight_ref.2) | copy-start | bytes 18436
  103.3 5.0 %copy-start.7 = (s32[2]{0:T(128)S(1)}, s32[2]{0:T(128)}, u32[]{:S(2)}) copy-start(s32[2]{0:T(128)} %size_hbm.3) | copy-start | bytes 28
  103.3 48.3 %all-to-all-start.1 = ((bf16[128,13,8,128]{3,2,1,0:T(8,128)(2,1)}), bf16[128,13,8,128]{3,2,1,0:T(8,128)(2,1)S(1)}, u32[]{:S(2)}, u32[]{:S(2)}) async-start(bf16[128,13,8,128]{3,2,1,0:T(8,128)(2,1)} %bitcast.2), calls=%async_computation.1 | async-start | bytes 6815744 | tf_op jit(solution)/shard_map/all_to_all | solution.py:323
  108.4 1.7 %copy-start.1 = (bf16[2,768,768]{2,1,0:T(8,128)(2,1)S(1)}, bf16[2,768,768]{2,1,0:T(8,128)(2,1)}, u32[]{:S(2)}) copy-start(bf16[2,768,768]{2,1,0:T(8,128)(2,1)} %gen_hbm.1) | copy-start | bytes 7077892
  110.0 1.7 %copy-start.2 = (bf16[2,768,768]{2,1,0:T(8,128)(2,1)S(1)}, bf16[2,768,768]{2,1,0:T(8,128)(2,1)}, u32[]{:S(2)}) copy-start(bf16[2,768,768]{2,1,0:T(8,128)(2,1)} %ham_hbm.1) | copy-start | bytes 7077892
  111.7 40.0 %copy-start.3 = (s32[1,1664]{1,0:T(1,128)S(1)}, s32[1,1664]{1,0:T(1,128)}, u32[]{:S(2)}) copy-start(s32[1,1664]{1,0:T(1,128)} %table.3) | copy-start | bytes 19972
  118.2 2.1 %copy-start = (f32[2,768,768]{2,1,0:T(8,128)}, f32[2,768,768]{2,1,0:T(8,128)S(1)}, u32[]{:S(2)}) copy-start(f32[2,768,768]{2,1,0:T(8,128)S(1)} %ladder.1.base_hbm) | copy-start | bytes 14155780

commit v6 on v5

--- a/solution.py
+++ b/solution.py
@@ -313,7 +313,7 @@
             pltpu.VMEM((channels, extent, extent), bf16),
             pltpu.VMEM((2 * lane_rows, LANES), f32),
             pltpu.SemaphoreType.DMA((3,)),
-            pltpu.SemaphoreType.DMA((2, 4 * channels)),
+            pltpu.SemaphoreType.DMA((2, 2 * channels)),
         ],
         compiler_params=params(PACK_MIB),
         name="pack",

time: 156 us -> 156 us (level)
  no operation moved by 1% of the time
where the time goes in v6:
time: 156 us
  blocking collectives  91.2 us (58%)
  waiting for transfers between devices  31.3 us (20%)
  Pallas kernels  22.4 us (14%)
  local copies, waits for them, and re-layouts  5.48 us (4%)
  starting transfers between devices  5.01 us (3%)
    all_to_all x1, blocking collectives, exchange(): lax.all_to_all(tiles.reshape(devices, slots // devices, *tiles.shape[1:])...  91.2 us
    all_to_all x1, waiting for transfers between devices, exchange(): lax.all_to_all(tiles.reshape(devices, slots // devices, *tiles.shape[1:])...  31.3 us
    pallas_call x1, Pallas kernels, per_device(): pl.pallas_call(cross_kernel, out_shape=jax.ShapeDtypeStruct((slots, TROWS...  7.96 us
    pallas_call x1, Pallas kernels, per_device(): pl.pallas_call(ladder_kernel, out_shape=jax.ShapeDtypeStruct((channels, e...  6.49 us
    unnamed x16, local copies, waits for them, and re-layouts  5.48 us
    all_to_all x1, starting transfers between devices, exchange(): lax.all_to_all(tiles.reshape(devices, slots // devices, *tiles.shape[1:])...  5.01 us
    pallas_call x1, Pallas kernels, per_device(): pl.pallas_call(finish_kernel, out_shape=jax.ShapeDtypeStruct((channels, e...  4.07 us
    pallas_call x1, Pallas kernels, per_device(): pl.pallas_call(pack_kernel, out_shape=jax.ShapeDtypeStruct((slots, 2 * TR...  3.91 us
  transfers between devices with their start and end apart: 1, of which 1 were waited for; matrix products, arithmetic and copies ran while one was open for 0% of the time, Pallas kernels for 4%

profile of v6, /device:TPU:1, one launch (start us, length us, event | category | flops | bytes accessed | tf_op | source)
XLA Modules:
  0.0 155.7 jit_solution(2853573027017876664)
XLA Ops:
  0.0 3.9 %pack.1 = bf16[1664,16,128]{2,1,0:T(8,128)(2,1)S(1)} custom-call(s32[2]{0:T(128)} %size_hbm.3, s32[1,1664]{1,0:T(1,128)} %table.3, bf16[2,768,768]{2,1,0:T(8,128)(2,1)} %gen_hbm.1, bf16[2,768,768]{2,1,0:T(8,128)(2,1)} %ham_hbm.1), custom_call_target="tpu_custom_call" | custom-call | tf_op jit(solution)/shard_map/pack/pallas_call | solution.py:302
  3.9 0.0 copy-start.4
  3.9 0.0 copy-start.5
  3.9 91.2 %all_to_all.10 = bf16[128,13,16,128]{3,2,1,0:T(8,128)(2,1)S(1)} all-to-all(bf16[128,13,16,128]{3,2,1,0:T(8,128)(2,1)S(1)} %bitcast.4), channel_id=1, replica_groups={{0,32,64,96,2,34,66,98,4,36,68,100,6,38,70,102,1,33,65,97,3,35,67,99,5,..., dimensions={0} | all-to-all | bytes 13631488 | tf_op jit(solution)/shard_map/all_to_all | solution.py:323
  95.1 0.0 copy-done.4
  95.1 0.0 copy-done.5
  95.1 8.0 %cross.1 = bf16[1664,8,128]{2,1,0:T(8,128)(2,1)} custom-call(s32[1,1664]{1,0:T(1,128)S(1)} %copy-done.4, f32[2,768]{1,0:T(2,128)S(1)} %copy-done.5, bf16[1664,16,128]{2,1,0:T(8,128)(2,1)S(1)} %bitcast.5), custom_call_target="tpu_custom_call" | custom-call | tf_op jit(solution)/shard_map/cross/pallas_call | solution.py:350
  103.1 0.0 copy-start.6
  103.1 0.0 copy-start.7
  103.1 5.0 %all-to-all-start.1 = ((bf16[128,13,8,128]{3,2,1,0:T(8,128)(2,1)}), bf16[128,13,8,128]{3,2,1,0:T(8,128)(2,1)S(1)}, u32[]{:S(2)}, u32[]{:S(2)}) async-start(bf16[128,13,8,128]{3,2,1,0:T(8,128)(2,1)} %bitcast.2), calls=%async_computation.1 | async-start | bytes 6815744 | tf_op jit(solution)/shard_map/all_to_all | solution.py:323
  108.1 0.0 copy-done.6
  108.1 0.0 copy-done.7
  108.1 0.0 copy-start.1
  108.1 1.7 %copy-done.1 = bf16[2,768,768]{2,1,0:T(8,128)(2,1)S(1)} copy-done((bf16[2,768,768]{2,1,0:T(8,128)(2,1)S(1)}, bf16[2,768,768]{2,1,0:T(8,128)(2,1)}, u32[]{:S(2)}) %copy-start.1) | copy-done | bytes 2359320
  109.8 0.0 copy-start.2
  109.8 1.7 %copy-done.2 = bf16[2,768,768]{2,1,0:T(8,128)(2,1)S(1)} copy-done((bf16[2,768,768]{2,1,0:T(8,128)(2,1)S(1)}, bf16[2,768,768]{2,1,0:T(8,128)(2,1)}, u32[]{:S(2)}) %copy-start.2) | copy-done | bytes 2359320
  111.5 0.0 copy-start.3
  111.5 6.5 %ladder.1.base_hbm = f32[2,768,768]{2,1,0:T(8,128)S(1)} custom-call(s32[2]{0:T(128)S(1)} %copy-done.7, f32[2,768]{1,0:T(2,128)S(1)} %copy-done.6, bf16[2,768,768]{2,1,0:T(8,128)(2,1)S(1)} %copy-done.1, bf16[2,768,768]{2,1,0:T(8,128)(2,1)S(1)} %copy-done.2), custom_call_target="tpu_custom_call" | custom-call | tf_op jit(solution)/shard_map/ladder/pallas_call | solution.py:335
  118.0 0.0 copy-start
  118.0 2.1 %copy-done = f32[2,768,768]{2,1,0:T(8,128)} copy-done((f32[2,768,768]{2,1,0:T(8,128)}, f32[2,768,768]{2,1,0:T(8,128)S(1)}, u32[]{:S(2)}) %copy-start) | copy-done | bytes 4718616
  120.1 31.3 %all-to-all-done.1 = bf16[128,13,8,128]{3,2,1,0:T(8,128)(2,1)S(1)} async-done(((bf16[128,13,8,128]{3,2,1,0:T(8,128)(2,1)}), bf16[128,13,8,128]{3,2,1,0:T(8,128)(2,1)S(1)}, u32[]{:S(2)}, u32[]{:S(2)}) %all-to-all-start.1) | async-done | bytes 3407904 | tf_op jit(solution)/shard_map/all_to_all | solution.py:323
  151.4 0.0 copy-done.3
  151.4 4.1 %finish.1 = f32[2,768,768]{2,1,0:T(8,128)} custom-call(s32[2]{0:T(128)S(1)} %copy-done.7, s32[1,1664]{1,0:T(1,128)S(1)} %copy-done.3, f32[2,768,768]{2,1,0:T(8,128)} %copy-done, bf16[1664,8,128]{2,1,0:T(8,128)(2,1)S(1)} %bitcast.6), custom_call_target="tpu_custom_call" | custom-call | tf_op jit(solution)/shard_map/finish/pallas_call | solution.py:371
Async XLA Ops:
  3.9 91.2 %copy-start.4 = (s32[1,1664]{1,0:T(1,128)S(1)}, s32[1,1664]{1,0:T(1,128)}, u32[]{:S(2)}) copy-start(s32[1,1664]{1,0:T(1,128)} %table.2) | copy-start | bytes 19972
  3.9 91.2 %copy-start.5 = (f32[2,768]{1,0:T(2,128)S(1)}, f32[2,768]{1,0:T(2,128)}, u32[]{:S(2)}) copy-start(f32[2,768]{1,0:T(2,128)} %weight_ref.3) | copy-start | bytes 18436
  103.1 5.0 %copy-start.6 = (f32[2,768]{1,0:T(2,128)S(1)}, f32[2,768]{1,0:T(2,128)}, u32[]{:S(2)}) copy-start(f32[2,768]{1,0:T(2,128)} %weight_ref.2) | copy-start | bytes 18436
  103.1 5.0 %copy-start.7 = (s32[2]{0:T(128)S(1)}, s32[2]{0:T(128)}, u32[]{:S(2)}) copy-start(s32[2]{0:T(128)} %size_hbm.3) | copy-start | bytes 28
  103.1 48.3 %all-to-all-start.1 = ((bf16[128,13,8,128]{3,2,1,0:T(8,128)(2,1)}), bf16[128,13,8,128]{3,2,1,0:T(8,128)(2,1)S(1)}, u32[]{:S(2)}, u32[]{:S(2)}) async-start(bf16[128,13,8,128]{3,2,1,0:T(8,128)(2,1)} %bitcast.2), calls=%async_computation.1 | async-start | bytes 6815744 | tf_op jit(solution)/shard_map/all_to_all | solution.py:323
  108.1 1.7 %copy-start.1 = (bf16[2,768,768]{2,1,0:T(8,128)(2,1)S(1)}, bf16[2,768,768]{2,1,0:T(8,128)(2,1)}, u32[]{:S(2)}) copy-start(bf16[2,768,768]{2,1,0:T(8,128)(2,1)} %gen_hbm.1) | copy-start | bytes 7077892
  109.8 1.7 %copy-start.2 = (bf16[2,768,768]{2,1,0:T(8,128)(2,1)S(1)}, bf16[2,768,768]{2,1,0:T(8,128)(2,1)}, u32[]{:S(2)}) copy-start(bf16[2,768,768]{2,1,0:T(8,128)(2,1)} %ham_hbm.1) | copy-start | bytes 7077892
  111.5 40.0 %copy-start.3 = (s32[1,1664]{1,0:T(1,128)S(1)}, s32[1,1664]{1,0:T(1,128)}, u32[]{:S(2)}) copy-start(s32[1,1664]{1,0:T(1,128)} %table.3) | copy-start | bytes 19972
  118.0 2.1 %copy-start = (f32[2,768,768]{2,1,0:T(8,128)}, f32[2,768,768]{2,1,0:T(8,128)S(1)}, u32[]{:S(2)}) copy-start(f32[2,768,768]{2,1,0:T(8,128)S(1)} %ladder.1.base_hbm) | copy-start | bytes 14155780

commit v7 on v6

--- a/solution.py
+++ b/solution.py
@@ -128,7 +128,7 @@
             body(place * capacity + k, pl.multiple_of(row, TROWS))
 
 
-def cross_kernel(table, weight_ref, arrived, out_hbm, words, first_rows, both_rows, gen, ham, wgen, wham, spread_weight, crossed_rows, out, small_sem, out_sem):
+def cross_kernel(table, weight_ref, arrived, out_hbm, words, first_rows, both_rows, left, right, spread_weight, crossed_rows, out, small_sem, out_sem):
     channels, extent = weight_ref.shape
     panels = extent // LANES
     other = both_rows.shape[0] // 2
@@ -167,13 +167,16 @@
                 both_rows[pl.ds(base + (other + p + i), ROWS, stride=panels), :]
                 for i in range(2)
             ]
-            for target, pair in (
-                (gen, g),
-                (ham, h),
-                (wgen, [weight * x for x in g]),
-                (wham, [weight * x for x in h]),
-            ):
-                target[c, rows, lanes] = jnp.concatenate(pair, axis=1).astype(jnp.bfloat16)
+            far = slice(extent + p * LANES, extent + (p + 2) * LANES)
+            below = pl.ds(first + extent, ROWS)
+
+            def joined(pair):
+                return jnp.concatenate(pair, axis=1).astype(jnp.bfloat16)
+
+            left[c, rows, lanes] = joined(g)
+            left[c, rows, far] = joined([-x for x in h])
+            right[c, rows, lanes] = joined([weight * x for x in h])
+            right[c, below, lanes] = joined([weight * x for x in g])
 
     def block(b):
         relayout(0, pl.multiple_of(b * ROWS, ROWS))
@@ -183,9 +186,7 @@
     for c in range(channels):
         for n in range(extent // step):
             columns = slice(n * step, (n + 1) * step)
-            first = jnp.dot(gen[c], wham[c, :, columns], preferred_element_type=jnp.float32)
-            second = jnp.dot(ham[c], wgen[c, :, columns], preferred_element_type=jnp.float32)
-            product = first - second
+            product = jnp.dot(left[c], right[c, :, columns], preferred_element_type=jnp.float32)
             for i in range(step // LANES):
                 p = n * (step // LANES) + i
                 crossed_rows[
@@ -354,7 +355,10 @@
         out_specs=HBM(),
         scratch_shapes=table_words
         + [pltpu.VMEM((2 * lane_rows, LANES), f32)]
-        + [pltpu.VMEM((channels, extent, extent), bf16)] * 4
+        + [
+            pltpu.VMEM((channels, extent, 2 * extent), bf16),
+            pltpu.VMEM((channels, 2 * extent, extent), bf16),
+        ]
         + [
             pltpu.VMEM((channels, extent, LANES), f32),
             pltpu.VMEM((lane_rows, LANES), f32),

time: 156 us -> 156 us (level)
  no operation moved by 1% of the time
where the time goes in v7:
time: 156 us
  blocking collectives  91.2 us (58%)
  waiting for transfers between devices  31.3 us (20%)
  Pallas kernels  22.6 us (14%)
  local copies, waits for them, and re-layouts  5.48 us (4%)
  starting transfers between devices  5.01 us (3%)
    all_to_all x1, blocking collectives, exchange(): lax.all_to_all(tiles.reshape(devices, slots // devices, *tiles.shape[1:])...  91.2 us
    all_to_all x1, waiting for transfers between devices, exchange(): lax.all_to_all(tiles.reshape(devices, slots // devices, *tiles.shape[1:])...  31.3 us
    pallas_call x1, Pallas kernels, per_device(): pl.pallas_call(cross_kernel, out_shape=jax.ShapeDtypeStruct((slots, TROWS...  8.11 us
    pallas_call x1, Pallas kernels, per_device(): pl.pallas_call(ladder_kernel, out_shape=jax.ShapeDtypeStruct((channels, e...  6.5 us
    unnamed x16, local copies, waits for them, and re-layouts  5.48 us
    all_to_all x1, starting transfers between devices, exchange(): lax.all_to_all(tiles.reshape(devices, slots // devices, *tiles.shape[1:])...  5.01 us
    pallas_call x1, Pallas kernels, per_device(): pl.pallas_call(finish_kernel, out_shape=jax.ShapeDtypeStruct((channels, e...  4.07 us
    pallas_call x1, Pallas kernels, per_device(): pl.pallas_call(pack_kernel, out_shape=jax.ShapeDtypeStruct((slots, 2 * TR...  3.91 us
  transfers between devices with their start and end apart: 1, of which 1 were waited for; matrix products, arithmetic and copies ran while one was open for 0% of the time, Pallas kernels for 4%

profile of v7, /device:TPU:1, one launch (start us, length us, event | category | flops | bytes accessed | tf_op | source)
XLA Modules:
  0.0 155.8 jit_solution(8893878976932551899)
XLA Ops:
  0.0 3.9 %pack.1 = bf16[1664,16,128]{2,1,0:T(8,128)(2,1)S(1)} custom-call(s32[2]{0:T(128)} %size_hbm.3, s32[1,1664]{1,0:T(1,128)} %table.3, bf16[2,768,768]{2,1,0:T(8,128)(2,1)} %gen_hbm.1, bf16[2,768,768]{2,1,0:T(8,128)(2,1)} %ham_hbm.1), custom_call_target="tpu_custom_call" | custom-call | tf_op jit(solution)/shard_map/pack/pallas_call | solution.py:303
  3.9 0.0 copy-start.4
  3.9 0.0 copy-start.5
  3.9 91.2 %all_to_all.10 = bf16[128,13,16,128]{3,2,1,0:T(8,128)(2,1)S(1)} all-to-all(bf16[128,13,16,128]{3,2,1,0:T(8,128)(2,1)S(1)} %bitcast.4), channel_id=1, replica_groups={{0,32,64,96,2,34,66,98,4,36,68,100,6,38,70,102,1,33,65,97,3,35,67,99,5,..., dimensions={0} | all-to-all | bytes 13631488 | tf_op jit(solution)/shard_map/all_to_all | solution.py:324
  95.1 0.0 copy-done.4
  95.1 0.0 copy-done.5
  95.1 8.1 %cross.1 = bf16[1664,8,128]{2,1,0:T(8,128)(2,1)} custom-call(s32[1,1664]{1,0:T(1,128)S(1)} %copy-done.4, f32[2,768]{1,0:T(2,128)S(1)} %copy-done.5, bf16[1664,16,128]{2,1,0:T(8,128)(2,1)S(1)} %bitcast.5), custom_call_target="tpu_custom_call" | custom-call | tf_op jit(solution)/shard_map/cross/pallas_call | solution.py:351
  103.2 0.0 copy-start.6
  103.2 0.0 copy-start.7
  103.2 5.0 %all-to-all-start.1 = ((bf16[128,13,8,128]{3,2,1,0:T(8,128)(2,1)}), bf16[128,13,8,128]{3,2,1,0:T(8,128)(2,1)S(1)}, u32[]{:S(2)}, u32[]{:S(2)}) async-start(bf16[128,13,8,128]{3,2,1,0:T(8,128)(2,1)} %bitcast.2), calls=%async_computation.1 | async-start | bytes 6815744 | tf_op jit(solution)/shard_map/all_to_all | solution.py:324
  108.3 0.0 copy-done.6
  108.3 0.0 copy-done.7
  108.3 0.0 copy-start.1
  108.3 1.7 %copy-done.1 = bf16[2,768,768]{2,1,0:T(8,128)(2,1)S(1)} copy-done((bf16[2,768,768]{2,1,0:T(8,128)(2,1)S(1)}, bf16[2,768,768]{2,1,0:T(8,128)(2,1)}, u32[]{:S(2)}) %copy-start.1) | copy-done | bytes 2359320
  109.9 0.0 copy-start.2
  109.9 1.7 %copy-done.2 = bf16[2,768,768]{2,1,0:T(8,128)(2,1)S(1)} copy-done((bf16[2,768,768]{2,1,0:T(8,128)(2,1)S(1)}, bf16[2,768,768]{2,1,0:T(8,128)(2,1)}, u32[]{:S(2)}) %copy-start.2) | copy-done | bytes 2359320
  111.6 0.0 copy-start.3
  111.6 6.5 %ladder.1.base_hbm = f32[2,768,768]{2,1,0:T(8,128)S(1)} custom-call(s32[2]{0:T(128)S(1)} %copy-done.7, f32[2,768]{1,0:T(2,128)S(1)} %copy-done.6, bf16[2,768,768]{2,1,0:T(8,128)(2,1)S(1)} %copy-done.1, bf16[2,768,768]{2,1,0:T(8,128)(2,1)S(1)} %copy-done.2), custom_call_target="tpu_custom_call" | custom-call | tf_op jit(solution)/shard_map/ladder/pallas_call | solution.py:336
  118.1 0.0 copy-start
  118.1 2.1 %copy-done = f32[2,768,768]{2,1,0:T(8,128)} copy-done((f32[2,768,768]{2,1,0:T(8,128)}, f32[2,768,768]{2,1,0:T(8,128)S(1)}, u32[]{:S(2)}) %copy-start) | copy-done | bytes 4718616
  120.2 31.3 %all-to-all-done.1 = bf16[128,13,8,128]{3,2,1,0:T(8,128)(2,1)S(1)} async-done(((bf16[128,13,8,128]{3,2,1,0:T(8,128)(2,1)}), bf16[128,13,8,128]{3,2,1,0:T(8,128)(2,1)S(1)}, u32[]{:S(2)}, u32[]{:S(2)}) %all-to-all-start.1) | async-done | bytes 3407904 | tf_op jit(solution)/shard_map/all_to_all | solution.py:324
  151.6 0.0 copy-done.3
  151.6 4.1 %finish.1 = f32[2,768,768]{2,1,0:T(8,128)} custom-call(s32[2]{0:T(128)S(1)} %copy-done.7, s32[1,1664]{1,0:T(1,128)S(1)} %copy-done.3, f32[2,768,768]{2,1,0:T(8,128)} %copy-done, bf16[1664,8,128]{2,1,0:T(8,128)(2,1)S(1)} %bitcast.6), custom_call_target="tpu_custom_call" | custom-call | tf_op jit(solution)/shard_map/finish/pallas_call | solution.py:375
Async XLA Ops:
  3.9 91.2 %copy-start.4 = (s32[1,1664]{1,0:T(1,128)S(1)}, s32[1,1664]{1,0:T(1,128)}, u32[]{:S(2)}) copy-start(s32[1,1664]{1,0:T(1,128)} %table.2) | copy-start | bytes 19972
  3.9 91.2 %copy-start.5 = (f32[2,768]{1,0:T(2,128)S(1)}, f32[2,768]{1,0:T(2,128)}, u32[]{:S(2)}) copy-start(f32[2,768]{1,0:T(2,128)} %weight_ref.3) | copy-start | bytes 18436
  103.2 5.0 %copy-start.6 = (f32[2,768]{1,0:T(2,128)S(1)}, f32[2,768]{1,0:T(2,128)}, u32[]{:S(2)}) copy-start(f32[2,768]{1,0:T(2,128)} %weight_ref.2) | copy-start | bytes 18436
  103.2 5.0 %copy-start.7 = (s32[2]{0:T(128)S(1)}, s32[2]{0:T(128)}, u32[]{:S(2)}) copy-start(s32[2]{0:T(128)} %size_hbm.3) | copy-start | bytes 28
  103.2 48.3 %all-to-all-start.1 = ((bf16[128,13,8,128]{3,2,1,0:T(8,128)(2,1)}), bf16[128,13,8,128]{3,2,1,0:T(8,128)(2,1)S(1)}, u32[]{:S(2)}, u32[]{:S(2)}) async-start(bf16[128,13,8,128]{3,2,1,0:T(8,128)(2,1)} %bitcast.2), calls=%async_computation.1 | async-start | bytes 6815744 | tf_op jit(solution)/shard_map/all_to_all | solution.py:324
  108.3 1.7 %copy-start.1 = (bf16[2,768,768]{2,1,0:T(8,128)(2,1)S(1)}, bf16[2,768,768]{2,1,0:T(8,128)(2,1)}, u32[]{:S(2)}) copy-start(bf16[2,768,768]{2,1,0:T(8,128)(2,1)} %gen_hbm.1) | copy-start | bytes 7077892
  109.9 1.7 %copy-start.2 = (bf16[2,768,768]{2,1,0:T(8,128)(2,1)S(1)}, bf16[2,768,768]{2,1,0:T(8,128)(2,1)}, u32[]{:S(2)}) copy-start(bf16[2,768,768]{2,1,0:T(8,128)(2,1)} %ham_hbm.1) | copy-start | bytes 7077892
  111.6 40.0 %copy-start.3 = (s32[1,1664]{1,0:T(1,128)S(1)}, s32[1,1664]{1,0:T(1,128)}, u32[]{:S(2)}) copy-start(s32[1,1664]{1,0:T(1,128)} %table.3) | copy-start | bytes 19972
  118.1 2.1 %copy-start = (f32[2,768,768]{2,1,0:T(8,128)}, f32[2,768,768]{2,1,0:T(8,128)S(1)}, u32[]{:S(2)}) copy-start(f32[2,768,768]{2,1,0:T(8,128)S(1)} %ladder.1.base_hbm) | copy-start | bytes 14155780
